TPU v7x, 32 devices: a whole 2x2x4 slice. The times are simulated.
32 devices in a mesh: groups: 2 (over y), seq: 16 (over z, x, core).
Axes of the slice: x: 2, y: 2, z: 4, core: 2. Of those that a mesh axis runs over, the one named last changes fastest.
Arguments:
- queries: bfloat16 [8192, 2048], P(('groups', 'seq')), parts along dimension 0, may hold values from -60 to 60
- keys: bfloat16 [8192, 1024], P(('groups', 'seq')), parts along dimension 0, may hold values from -6 to 6
- values: bfloat16 [8192, 1024], P(('groups', 'seq')), parts along dimension 0, may hold values from -6 to 6
- residual: bfloat16 [8192, 2688], P(('groups', 'seq')), parts along dimension 0, may hold values from -6 to 6
- out_weight: bfloat16 [2048, 2688], P('seq'), may hold values from -2 to 2
- post_scale: float32 [2688], replicated, may hold values from 0.5 to 2
- doc_starts: int32 [64], P('groups'), parts along dimension 0, may hold values from 0 to 4096, as said below
Outputs:
- hidden: bfloat16 [8192, 2688], P(('groups', 'seq')), parts along dimension 0
- pooled: float32 [64, 2688], P(('groups', 'seq')), parts along dimension 0
There are 2 independent parts, one for each index of `groups`. A program takes and returns all parts, laid end to end along the dimension named above; an argument that names none is the same for every part. Nothing has to cross between parts.
Inputs may be any that keep to these rules, and one draw needn't show every extreme that they name: `doc_starts`: entries k * 2 to (k + 1) * 2 - 1 hold, rising, the positions in [k * 256, (k + 1) * 256) at which documents start, followed by (k + 1) * 256 in unused entries. Entry 0 is 0. Some device has 2 starts.
All inputs are finite; a program needn't handle non-finite values.
Results may differ from a plain program's by a relative error of at most 0.0051.
Values may be sent and summed in bfloat16 or wider, within the bound.
No kernel may reach another device: no remote copies, remote signals or barrier semaphores. Data moves between devices by JAX's collectives and lax.ppermute only.
A program may use at most 64 MiB of HBM per device.

v0:
```python
import math

import jax
import jax.numpy as jnp
from jax import lax
from jax.experimental import pallas as pl
from jax.experimental.pallas import tpu as pltpu
from jax.sharding import PartitionSpec as P


HEAD_FEATURES = 128
WINDOW_SPAN = 1024
SLOTS = 2
LANES = 128
UNUSED = 2**30

query_scale = 168.0 ** (-0.5)
norm_eps = 1e-06


def chip_grid(mesh):
    devices = mesh.devices.reshape(mesh.shape["groups"], mesh.shape["seq"])
    where = [(*d.coords, d.core_on_chip) for d in devices[0]]
    xs = len({w[0] for w in where})
    zs = len({w[2] for w in where})
    if xs * zs * 2 != len(where):
        return None
    return zs, xs


def passed_along(block, axis, distance):
    devices = range(lax.axis_size(axis))
    route = [(i - distance, i) for i in devices if i - distance in devices]
    return lax.ppermute(block, axis, route)


def moved(block, grid, step):
    zs, xs = grid
    route = []
    for z in range(zs):
        for x in range(xs):
            for c in range(2):
                to = step(z, x, c)
                if to is not None:
                    route.append(((z * xs + x) * 2 + c, (to[0] * xs + to[1]) * 2 + to[2]))
    return lax.ppermute(block, "seq", route)


def last_start_at(pos, prev, s0, s1):
    last = jnp.maximum(prev, jnp.where(s0 <= pos, s0, 0))
    return jnp.maximum(last, jnp.where(s1 <= pos, s1, 0))


def attend(meta, queries, key_blocks, value_blocks, block_at, heads_from, heads_to, per_step):
    rows, width = queries.shape
    kv_width = key_blocks[0].shape[1]
    each = width // kv_width
    count = len(key_blocks)
    tall = each * rows
    to_exp2 = query_scale * math.log2(math.e)
    steps = (heads_to - heads_from) // per_step
    skip = heads_from // per_step

    def kernel(meta, q_ref, *refs):
        k_refs, v_refs = refs[:count], refs[count : 2 * count]
        out_ref, bias, s_ref, m_ref, l_ref, acc = refs[2 * count :]
        first = meta[0] * rows
        prev, s0, s1 = meta[1], meta[2], meta[3]
        lowest = jnp.maximum(last_start_at(first, prev, s0, s1), first - WINDOW_SPAN + 1)
        places = []
        for b in range(count):
            index, valid = block_at(b, meta[0])
            start = index * rows
            places.append((start, valid & (index >= 0) & (start + rows > lowest)))

        @pl.when(pl.program_id(0) == 0)
        def _():
            for b, (start, need) in enumerate(places):

                @pl.when(need)
                def _():
                    q_pos = first + lax.broadcasted_iota(jnp.int32, (rows, rows), 0)
                    k_pos = start + lax.broadcasted_iota(jnp.int32, (rows, rows), 1)
                    low = last_start_at(q_pos, prev, s0, s1)
                    low = jnp.maximum(low, q_pos - WINDOW_SPAN + 1)
                    visible = (k_pos >= low) & (k_pos <= q_pos)
                    bias[b] = jnp.where(visible, 0.0, -jnp.inf)

        m_ref[...] = jnp.full(m_ref.shape, -jnp.inf, jnp.float32)
        l_ref[...] = jnp.zeros(l_ref.shape, jnp.float32)
        acc[...] = jnp.zeros(acc.shape, jnp.float32)

        def lanes(block):
            return [block[:, t : t + LANES] for t in range(0, rows, LANES)]

        for b, (start, need) in enumerate(places):

            @pl.when(need)
            def _():
                for g in range(per_step):
                    k = k_refs[b][:, g * HEAD_FEATURES : (g + 1) * HEAD_FEATURES]
                    for r in range(each):
                        at = (g * each + r) * HEAD_FEATURES
                        s = lax.dot_general(
                            q_ref[:, at : at + HEAD_FEATURES], k,
                            (((1,), (1,)), ((), ())), preferred_element_type=jnp.float32,
                        )
                        s = s + bias[b]
                        s_ref[b, g, r * rows : (r + 1) * rows] = s
                        top = m_ref[g, r * rows : (r + 1) * rows]
                        for part in lanes(s):
                            top = jnp.maximum(top, part)
                        m_ref[g, r * rows : (r + 1) * rows] = top

        for g in range(per_step):
            peak = jnp.max(m_ref[g], axis=1, keepdims=True)
            m_ref[g] = jnp.broadcast_to(peak, (tall, LANES))

        for b, (start, need) in enumerate(places):

            @pl.when(need)
            def _():
                for g in range(per_step):
                    peak = m_ref[g]
                    parts = [jnp.exp2((part - peak) * to_exp2) for part in lanes(s_ref[b, g])]
                    l_ref[g] += sum(parts[1:], parts[0])
                    p = jnp.concatenate([part.astype(jnp.bfloat16) for part in parts], axis=1)
                    acc[g] += jnp.dot(
                        p,
                        v_refs[b][:, g * HEAD_FEATURES : (g + 1) * HEAD_FEATURES],
                        preferred_element_type=jnp.float32,
                    )

        for g in range(per_step):
            totals = jnp.sum(l_ref[g], axis=1, keepdims=True)
            result = (acc[g] / totals).astype(jnp.bfloat16)
            for r in range(each):
                at = (g * each + r) * HEAD_FEATURES
                out_ref[:, at : at + HEAD_FEATURES] = result[r * rows : (r + 1) * rows]

    q_spec = pl.BlockSpec((rows, per_step * each * HEAD_FEATURES), lambda g, meta: (0, g + skip))
    kv_spec = pl.BlockSpec((rows, per_step * HEAD_FEATURES), lambda g, meta: (0, g + skip))
    out_spec = pl.BlockSpec((rows, per_step * each * HEAD_FEATURES), lambda g, meta: (0, g))
    return pl.pallas_call(
        kernel,
        grid_spec=pltpu.PrefetchScalarGridSpec(
            num_scalar_prefetch=1,
            grid=(steps,),
            in_specs=[q_spec] + [kv_spec] * (2 * count),
            out_specs=out_spec,
            scratch_shapes=[
                pltpu.VMEM((count, rows, rows), jnp.float32),
                pltpu.VMEM((count, per_step, tall, rows), jnp.float32),
                pltpu.VMEM((per_step, tall, LANES), jnp.float32),
                pltpu.VMEM((per_step, tall, LANES), jnp.float32),
                pltpu.VMEM((per_step, tall, HEAD_FEATURES), jnp.float32),
            ],
        ),
        out_shape=jax.ShapeDtypeStruct((rows, steps * per_step * each * HEAD_FEATURES), jnp.bfloat16),
        name="attend",
    )(meta, queries, *key_blocks, *value_blocks)


def gathered(refs, w_ref, offs, sems):
    copies = []
    for i, ref in enumerate(refs):
        tall = ref.shape[0]
        at = pl.multiple_of(offs[i], math.gcd(tall, 16))
        copies.append(pltpu.make_async_copy(ref, w_ref.at[pl.ds(at, tall)], sems.at[i]))
    return copies


def column_split(columns):
    tiles = columns // LANES
    return next(n for n in (3, 2, 1) if tiles % n == 0) * LANES


def project_early(chunk_at, attended, pieces, offsets, chunk):
    rows = attended.shape[0]
    columns = pieces[0].shape[1]
    count = len(pieces)
    chunks = chunk_at.shape[0]
    split = column_split(columns)

    def kernel(chunk_at, offs, att_ref, *refs):
        piece_refs = refs[:count]
        out_ref, w_ref, att, sems = refs[count:]
        copies = gathered(piece_refs, w_ref, offs, sems)
        for copy in copies:
            copy.start()
        for i in range(chunks):
            at = pl.multiple_of(chunk_at[i] * chunk, LANES)
            att[:, i * chunk : (i + 1) * chunk] = att_ref[:, pl.ds(at, chunk)]
        for copy in copies:
            copy.wait()
        for at in range(0, columns, split):
            out_ref[:, at : at + split] = jnp.dot(
                att[...], w_ref[:, at : at + split], preferred_element_type=jnp.float32
            )

    whole = pl.BlockSpec(memory_space=pltpu.MemorySpace.VMEM)
    smem = pl.BlockSpec(memory_space=pltpu.MemorySpace.SMEM)
    return pl.pallas_call(
        kernel,
        in_specs=[smem, smem, whole] + [pl.BlockSpec(memory_space=pl.ANY)] * count,
        out_specs=whole,
        out_shape=jax.ShapeDtypeStruct((rows, columns), jnp.float32),
        scratch_shapes=[
            pltpu.VMEM((chunks * chunk, columns), jnp.bfloat16),
            pltpu.VMEM((rows, chunks * chunk), jnp.bfloat16),
            pltpu.SemaphoreType.DMA((count,)),
        ],
        name="project_early",
    )(chunk_at, offsets, attended, *pieces)


def project(meta, chunk_at, chunk, attended, partial, residual, post_scale, pieces, offsets, seq_size):
    rows = attended.shape[0]
    columns = residual.shape[1]
    count = len(pieces)
    tiles = columns // LANES
    padded = -(-tiles // 8) * 8
    split = column_split(columns)
    starts = range(0, columns, split)
    partials = [] if partial is None else [partial]

    def kernel(meta, chunk_at, offs, att_ref, res_ref, post_ref, *refs):
        part_refs, refs = refs[: len(partials)], refs[len(partials) :]
        piece_refs = refs[:count]
        hidden_ref, sums_ref, send_ref, w_ref, proj, sems = refs[count:]
        copies = gathered(piece_refs, w_ref, offs, sems)
        for copy in copies:
            copy.start()
        first = meta[0] * rows
        prev, s0, s1 = meta[1], meta[2], meta[3]
        send_ref[...] = jnp.zeros(send_ref.shape, jnp.float32)
        pos = first + lax.broadcasted_iota(jnp.int32, (8, rows), 1)
        line = lax.broadcasted_iota(jnp.int32, (8, rows), 0)
        last = last_start_at(pos, prev, s0, s1)
        masks = (
            ((line == 0) & (last == s0)) | ((line == 1) & (last == s1)) | ((line == 2) & (last < first))
        ).astype(jnp.float32)
        att = att_ref[:, pl.ds(pl.multiple_of(chunk_at[0] * chunk, LANES), chunk)]
        for copy in copies:
            copy.wait()
        square = jnp.zeros((rows, LANES), jnp.float32)
        for at in starts:
            part = jnp.dot(att, w_ref[:, at : at + split], preferred_element_type=jnp.float32)
            for ref in part_refs:
                part = part + ref[:, at : at + split]
            proj[:, at : at + split] = part
            for t in range(0, split, LANES):
                square = square + part[:, t : t + LANES] * part[:, t : t + LANES]
        total = jnp.sum(square, axis=1, keepdims=True)
        norm = jnp.broadcast_to(lax.rsqrt(total * (1.0 / columns) + norm_eps), (rows, LANES))
        norm = jnp.concatenate([norm] * (split // LANES), axis=1)
        owner = prev // rows
        for at in starts:
            updated = res_ref[:, at : at + split].astype(jnp.float32) + (
                proj[:, at : at + split] * norm * post_ref[:, at : at + split]
            )
            hidden_ref[:, at : at + split] = updated.astype(jnp.bfloat16)
            sums = jnp.dot(
                masks, updated, precision=lax.Precision.HIGHEST, preferred_element_type=jnp.float32
            )
            sums_ref[:, at : at + split] = sums
            for t in range(split // LANES):
                send_ref[pl.ds(owner, 1), at // LANES + t, :] = sums[
                    2:3, t * LANES : (t + 1) * LANES
                ]

    whole = pl.BlockSpec(memory_space=pltpu.MemorySpace.VMEM)
    smem = pl.BlockSpec(memory_space=pltpu.MemorySpace.SMEM)
    return pl.pallas_call(
        kernel,
        in_specs=[smem, smem, smem, whole, whole, whole]
        + [whole] * len(partials)
        + [pl.BlockSpec(memory_space=pl.ANY)] * count,
        out_specs=(whole, whole, whole),
        out_shape=(
            jax.ShapeDtypeStruct((rows, columns), jnp.bfloat16),
            jax.ShapeDtypeStruct((8, columns), jnp.float32),
            jax.ShapeDtypeStruct((seq_size, padded, LANES), jnp.float32),
        ),
        scratch_shapes=[
            pltpu.VMEM((chunk, columns), jnp.bfloat16),
            pltpu.VMEM((rows, columns), jnp.float32),
            pltpu.SemaphoreType.DMA((count,)),
        ],
        name="project",
    )(meta, chunk_at, offsets, attended, residual, post_scale[None, :], *partials, *pieces)


def by_links(grid, groups, tok_rows, part_rows):
    return grid == (4, 2) and groups == 2 and WINDOW_SPAN == 4 * tok_rows and part_rows % 32 == 0


def body(grid, queries, keys, values, residual, out_weight, post_scale, doc_starts):
    seq_size = lax.axis_size("seq")
    my_index = lax.axis_index("seq")
    tok_rows = queries.shape[0]
    halo_blocks = WINDOW_SPAN // tok_rows
    part_rows = out_weight.shape[0]
    kv_heads = keys.shape[1] // HEAD_FEATURES

    slot_count = doc_starts.shape[0]
    slot_ids = jnp.arange(slot_count, dtype=jnp.int32)
    live_slot = doc_starts < (slot_ids // SLOTS + 1) * tok_rows
    first = my_index * tok_rows
    my_starts = lax.dynamic_slice_in_dim(doc_starts, my_index * SLOTS, SLOTS)
    my_live = my_starts < first + tok_rows
    prev = jnp.max(jnp.where(live_slot & (doc_starts < first), doc_starts, 0))
    shown = jnp.where(my_live, my_starts, UNUSED)
    meta = jnp.concatenate([my_index[None], prev[None], shown]).astype(jnp.int32)

    if by_links(grid, lax.axis_size("groups"), tok_rows, part_rows):
        zs, xs = grid
        half_rows = part_rows // 2
        chunk = xs * 2 * part_rows
        z, x, c = my_index // 4, my_index // 2 % 2, my_index % 2
        y = lax.axis_index("groups")

        def turned(k):
            return lambda block: moved(block, grid, lambda z, x, c: ((z + k) % zs, x, c))

        def over_x(block):
            return moved(block, grid, lambda z, x, c: (z, 1 - x, c))

        def over_c(block):
            return moved(block, grid, lambda z, x, c: (z, x, 1 - c))

        def over_y(block):
            return lax.ppermute(block, "groups", [(0, 1), (1, 0)])

        def up(block):
            return moved(block, grid, lambda z, x, c: (z + 1, x, c) if z + 1 < zs else None)

        def right(block):
            return moved(block, grid, lambda z, x, c: (z, x, 1) if c == 0 else None)

        def left(block):
            return moved(block, grid, lambda z, x, c: (z, x, 0) if c == 1 else None)

        own = lax.dynamic_slice_in_dim(out_weight, y * half_rows, half_rows)
        early, late = ([], []), ([], [])

        def place(which, slot, piece, x, c, half):
            which[0].append(piece)
            which[1].append((slot * xs * 2 + x * 2 + c) * part_rows + half * half_rows)

        def place_all(which, slot, piece, x):
            other = over_y(piece)
            place(which, slot, piece, x, c, y)
            place(which, slot, other, x, c, 1 - y)
            place(which, slot, over_c(piece), x, 1 - c, y)
            place(which, slot, over_c(other), x, 1 - c, 1 - y)

        place(early, 0, out_weight, x, c, 0)
        place(early, 0, over_c(out_weight), x, 1 - c, 0)
        place_all(early, 0, over_x(own), 1 - x)
        for slot, k in ((1, 1), (2, 3), (0, 2)):
            which = late if k == 2 else early
            ring = turned(k)(own)
            place_all(which, slot, ring, x)
            place_all(which, slot, over_x(ring), 1 - x)
        early_at = jnp.stack([z, (z - 1) % zs, (z - 3) % zs]).astype(jnp.int32)
        late_at = ((z - 2) % zs)[None].astype(jnp.int32)
        early_offsets = jnp.stack([jnp.asarray(o, jnp.int32) for o in early[1]])
        late_offsets = jnp.stack([jnp.asarray(o, jnp.int32) for o in late[1]])

        groups = []
        for mine in (keys, values):
            below = up(mine)
            aside = over_x(jnp.where(x == 0, mine, below))
            groups.append([mine, right(mine), below, left(below), aside, over_c(aside)])
        key_blocks, value_blocks = groups

        def block_at(b, index):
            chip, core = index // 2, index % 2
            back = (0, 0, 2, 2, 1, 1)[b]
            place = (chip - back) * 2 + (core if b % 2 == 0 else 1 - core)
            valid = True
            if b == 1:
                valid = core == 1
            if b == 3:
                valid = core == 0
            return place, (place <= index) & valid

        attended = attend(
            meta, queries, key_blocks, value_blocks, block_at, 0, kv_heads, 4
        )
        partial = project_early(early_at, attended, early[0], early_offsets, chunk)
        pieces, offsets = late[0], late_offsets
    else:
        pieces = [lax.all_gather(out_weight, "seq", axis=0, tiled=True)]
        offsets = jnp.zeros((1,), jnp.int32)
        late_at, chunk, partial = offsets, out_weight.shape[0] * seq_size, None
        key_blocks, value_blocks = [keys], [values]
        for distance in range(1, halo_blocks + 1):
            key_blocks.append(passed_along(keys, "seq", distance))
            value_blocks.append(passed_along(values, "seq", distance))

        def block_at(b, index):
            return index - b, index >= b

        attended = attend(
            meta, queries, key_blocks, value_blocks, block_at, 0, kv_heads, math.gcd(kv_heads, 4)
        )

    hidden, slot_sums, send = project(
        meta, late_at, chunk, attended, partial, residual, post_scale, pieces, offsets, seq_size
    )
    arrived = lax.all_to_all(send, "seq", 0, 0, tiled=True)
    columns = residual.shape[1]
    carried_sum = jnp.sum(arrived, axis=0).reshape(-1)[:columns]
    last_live = jnp.sum(my_live.astype(jnp.int32)) - 1
    tail_pick = (jnp.arange(SLOTS, dtype=jnp.int32) == last_live).astype(jnp.float32)
    doc_sums = slot_sums[:SLOTS] + tail_pick[:, None] * carried_sum[None, :]
    total_tokens = tok_rows * seq_size
    later_starts = live_slot[None, :] & (doc_starts[None, :] > my_starts[:, None])
    following = jnp.min(jnp.where(later_starts, doc_starts[None, :], total_tokens), axis=1)
    doc_length = jnp.maximum(following - my_starts, 1).astype(jnp.float32)
    pooled = jnp.where(my_live[:, None], doc_sums / doc_length[:, None], 0.0)
    return (hidden, pooled)


def solution(mesh):
    grid = chip_grid(mesh)
    placed = (
        P(("groups", "seq"), None),
        P(("groups", "seq"), None),
        P(("groups", "seq"), None),
        P(("groups", "seq"), None),
        P("seq", None),
        P(),
        P("groups"),
    )

    def whole(*args):
        return body(grid, *args)

    step = jax.shard_map(
        whole,
        mesh=mesh,
        in_specs=placed,
        out_specs=(P(("groups", "seq"), None), P(("groups", "seq"), None)),
        check_vma=False,
    )

    def run(queries, keys, values, residual, out_weight, post_scale, doc_starts):
        args = (queries, keys, values, residual, out_weight, post_scale, doc_starts)
        return step(*args)

    return run
```

profile of v0, /device:TPU:0, one launch (start us, length us, event | category | flops | bytes accessed | tf_op | source)
XLA Modules:
  0.0 170.1 jit_solution(15608374865914528639)
XLA Ops:
  1.7 3.1 %collective-permute-start.15 = (bf16[64,2688]{1,0:T(8,128)(2,1)S(1)}, bf16[64,2688]{1,0:T(8,128)(2,1)}, u32[]{:S(2)}, u32[]{:S(2)}) collective-permute-start(bf16[64,2688]{1,0:T(8,128)(2,1)S(1)} %constant_dynamic-slice_fusion), channel_id=1, source_target_pairs={{0,4},{1,5},{2,6},{3,7},{4,8},{5,9},{6,10},{7,11},{8,12},{9,13},{1... | collective-permute-start | bytes 1032200 | tf_op jit(solution)/shard_map/ppermute | solution.py:46
  4.8 2.1 %collective-permute-start.23 = (bf16[64,2688]{1,0:T(8,128)(2,1)S(1)}, bf16[64,2688]{1,0:T(8,128)(2,1)}, u32[]{:S(2)}, u32[]{:S(2)}) collective-permute-start(bf16[64,2688]{1,0:T(8,128)(2,1)S(1)} %constant_dynamic-slice_fusion), channel_id=1, source_target_pairs={{0,12},{1,13},{2,14},{3,15},{4,0},{5,1},{6,2},{7,3},{8,4},{9,5},{1... | collective-permute-start | bytes 1032200 | tf_op jit(solution)/shard_map/ppermute | solution.py:46
  6.9 1.6 collective-permute-start.11
  8.6 1.7 %collective-permute-start.1 = (bf16[256,1024]{1,0:T(8,128)(2,1)}, bf16[256,1024]{1,0:T(8,128)(2,1)S(1)}, u32[]{:S(2)}, u32[]{:S(2)}) collective-permute-start(bf16[256,1024]{1,0:T(8,128)(2,1)} %refs_0_.2), channel_id=1, source_target_pairs={{0,4},{1,5},{2,6},{3,7},{4,8},{5,9},{6,10},{7,11},{8,12},{9,13},{1... | collective-permute-start | bytes 1572872 | tf_op jit(solution)/shard_map/ppermute | solution.py:46
  10.3 3.5 %collective-permute-start.6 = (bf16[256,1024]{1,0:T(8,128)(2,1)}, bf16[256,1024]{1,0:T(8,128)(2,1)S(1)}, u32[]{:S(2)}, u32[]{:S(2)}) collective-permute-start(bf16[256,1024]{1,0:T(8,128)(2,1)} %refs_6_.1), channel_id=1, source_target_pairs={{0,4},{1,5},{2,6},{3,7},{4,8},{5,9},{6,10},{7,11},{8,12},{9,13},{1... | collective-permute-start | bytes 1572872 | tf_op jit(solution)/shard_map/ppermute | solution.py:46
  13.8 2.1 %collective-permute-done.15.refs_6_ = bf16[64,2688]{1,0:T(8,128)(2,1)} collective-permute-done((bf16[64,2688]{1,0:T(8,128)(2,1)S(1)}, bf16[64,2688]{1,0:T(8,128)(2,1)}, u32[]{:S(2)}, u32[]{:S(2)}) %collective-permute-start.15) | collective-permute-done | bytes 344096 | tf_op jit(solution)/shard_map/ppermute | solution.py:46
  17.2 4.6 %collective-permute-done.23.refs_14_ = bf16[64,2688]{1,0:T(8,128)(2,1)} collective-permute-done((bf16[64,2688]{1,0:T(8,128)(2,1)S(1)}, bf16[64,2688]{1,0:T(8,128)(2,1)}, u32[]{:S(2)}, u32[]{:S(2)}) %collective-permute-start.23) | collective-permute-done | bytes 344096 | tf_op jit(solution)/shard_map/ppermute | solution.py:46
  21.8 3.8 %collective-permute-start.31 = (bf16[64,2688]{1,0:T(8,128)(2,1)S(1)}, bf16[64,2688]{1,0:T(8,128)(2,1)}, u32[]{:S(2)}, u32[]{:S(2)}) collective-permute-start(bf16[64,2688]{1,0:T(8,128)(2,1)S(1)} %constant_dynamic-slice_fusion), channel_id=1, source_target_pairs={{0,8},{1,9},{2,10},{3,11},{4,12},{5,13},{6,14},{7,15},{8,0},{9,1},... | collective-permute-start | bytes 1032200 | tf_op jit(solution)/shard_map/ppermute | solution.py:46
  27.0 22.5 %collective-permute-done.31.refs_1_ = bf16[64,2688]{1,0:T(8,128)(2,1)} collective-permute-done((bf16[64,2688]{1,0:T(8,128)(2,1)S(1)}, bf16[64,2688]{1,0:T(8,128)(2,1)}, u32[]{:S(2)}, u32[]{:S(2)}) %collective-permute-start.31) | collective-permute-done | bytes 344096 | tf_op jit(solution)/shard_map/ppermute | solution.py:46
  49.4 1.5 collective-permute-start.19
  51.5 1.5 collective-permute-start.16
  53.5 7.2 %collective-permute-done.19.refs_10_ = bf16[64,2688]{1,0:T(8,128)(2,1)} collective-permute-done((bf16[64,2688]{1,0:T(8,128)(2,1)}, bf16[64,2688]{1,0:T(8,128)(2,1)}, u32[]{:S(2)}, u32[]{:S(2)}) %collective-permute-start.19) | collective-permute-done | bytes 344096 | tf_op jit(solution)/shard_map/ppermute | solution.py:46
  60.7 1.5 collective-permute-start.12
  62.2 3.9 %collective-permute-done.27.refs_18_ = bf16[64,2688]{1,0:T(8,128)(2,1)} collective-permute-done((bf16[64,2688]{1,0:T(8,128)(2,1)}, bf16[64,2688]{1,0:T(8,128)(2,1)}, u32[]{:S(2)}, u32[]{:S(2)}) %collective-permute-start.27) | collective-permute-done | bytes 344096 | tf_op jit(solution)/shard_map/ppermute | solution.py:46
  66.6 3.5 %collective-permute-done.24.refs_15_ = bf16[64,2688]{1,0:T(8,128)(2,1)} collective-permute-done((bf16[64,2688]{1,0:T(8,128)(2,1)}, bf16[64,2688]{1,0:T(8,128)(2,1)}, u32[]{:S(2)}, u32[]{:S(2)}) %collective-permute-start.24) | collective-permute-done | bytes 344096 | tf_op jit(solution)/shard_map/ppermute | solution.py:333
  70.1 4.8 %collective-permute-done.12.refs_3_ = bf16[64,2688]{1,0:T(8,128)(2,1)} collective-permute-done((bf16[64,2688]{1,0:T(8,128)(2,1)}, bf16[64,2688]{1,0:T(8,128)(2,1)}, u32[]{:S(2)}, u32[]{:S(2)}) %collective-permute-start.12) | collective-permute-done | bytes 344096 | tf_op jit(solution)/shard_map/ppermute | solution.py:333
  76.4 1.5 collective-permute-start.32
  78.5 1.5 collective-permute-start.28
  81.2 1.6 collective-permute-done.35.refs_5_
  82.9 4.7 %collective-permute-done.32.refs_2_ = bf16[64,2688]{1,0:T(8,128)(2,1)S(1)} collective-permute-done((bf16[64,2688]{1,0:T(8,128)(2,1)}, bf16[64,2688]{1,0:T(8,128)(2,1)S(1)}, u32[]{:S(2)}, u32[]{:S(2)}) %collective-permute-start.32) | collective-permute-done | bytes 344096 | tf_op jit(solution)/shard_map/ppermute | solution.py:333
  88.1 6.8 %collective-permute-done.20.refs_11_ = bf16[64,2688]{1,0:T(8,128)(2,1)S(1)} collective-permute-done((bf16[64,2688]{1,0:T(8,128)(2,1)}, bf16[64,2688]{1,0:T(8,128)(2,1)S(1)}, u32[]{:S(2)}, u32[]{:S(2)}) %collective-permute-start.20) | collective-permute-done | bytes 344096 | tf_op jit(solution)/shard_map/ppermute | solution.py:333
  95.5 3.2 %collective-permute-done.28.refs_19_ = bf16[64,2688]{1,0:T(8,128)(2,1)S(1)} collective-permute-done((bf16[64,2688]{1,0:T(8,128)(2,1)}, bf16[64,2688]{1,0:T(8,128)(2,1)S(1)}, u32[]{:S(2)}, u32[]{:S(2)}) %collective-permute-start.28) | collective-permute-done | bytes 344096 | tf_op jit(solution)/shard_map/ppermute | solution.py:333
  100.5 1.5 collective-permute-start.36
  104.7 2.0 %collective-permute-start.4 = (bf16[256,1024]{1,0:T(8,128)(2,1)S(1)}, bf16[256,1024]{1,0:T(8,128)(2,1)}, u32[]{:S(2)}, u32[]{:S(2)}) collective-permute-start(bf16[256,1024]{1,0:T(8,128)(2,1)S(1)} %collective-permute-done.3.refs_4_), channel_id=1, source_target_pairs={{0,1},{1,0},{2,3},{3,2},{4,5},{5,4},{6,7},{7,6},{8,9},{9,8},{10,11... | collective-permute-start | bytes 1572872 | tf_op jit(solution)/shard_map/ppermute | solution.py:46
  106.7 1.9 %collective-permute-done.8.refs_10_ = bf16[256,1024]{1,0:T(8,128)(2,1)S(1)} collective-permute-done((bf16[256,1024]{1,0:T(8,128)(2,1)S(1)}, bf16[256,1024]{1,0:T(8,128)(2,1)S(1)}, u32[]{:S(2)}, u32[]{:S(2)}) %collective-permute-start.8) | collective-permute-done | bytes 524320 | tf_op jit(solution)/shard_map/ppermute | solution.py:46
  109.4 1.5 collective-permute-done.36.refs_6_
  117.1 7.3 %attend.1.att_ref = bf16[256,2048]{1,0:T(8,128)(2,1)} custom-call(s32[4]{0:T(128)} %pad_add_fusion.meta, bf16[256,2048]{1,0:T(8,128)(2,1)} %q_ref.1, bf16[256,1024]{1,0:T(8,128)(2,1)} %refs_0_.2, bf16[256,1024]{1,0:T(8,128)(2,1)} %copy-done.4, bf16[256,1024]{1,0:T(8,128)(2,1)} %copy-done.1, bf16[256,1024]{1,0:T(8,128)(2,1)} %copy-done.8, ...), custom_call_target="tpu_custom_call" | custom-call | tf_op jit(solution)/shard_map/attend/pallas_call | solution.py:144
  124.5 9.3 %project_early.1.refs_0_ = f32[256,2688]{1,0:T(8,128)} custom-call(s32[3]{0:T(128)} %pad_add_fusion.1.chunk_at, s32[22]{0:T(128)} %stack.131.offs, bf16[256,2048]{1,0:T(8,128)(2,1)} %attend.1.att_ref, bf16[128,2688]{1,0:T(8,128)(2,1)} %refs_0_.3, bf16[128,2688]{1,0:T(8,128)(2,1)} %copy-done.3, bf16[64,2688]{1,0:T(8,128)(2,1)} %collective-permute-done.11.refs_2_, ...), custom_call_target="tpu_custom_call" | custom-call | tf_op jit(solution)/shard_map/project_early/pallas_call | solution.py:203
  134.6 7.9 %project.1 = (bf16[256,2688]{1,0:T(8,128)(2,1)}, f32[8,2688]{1,0:T(8,128)}, f32[16,24,128]{2,1,0:T(8,128)}) custom-call(s32[4]{0:T(128)} %pad_add_fusion.meta, s32[1]{0:T(128)} %bitcast.2.chunk_at, s32[8]{0:T(128)} %stack.108.offs, bf16[256,2048]{1,0:T(8,128)(2,1)} %attend.1.att_ref, bf16[256,2688]{1,0:T(8,128)(2,1)} %res_ref.1, ...), custom_call_target="tpu_custom_call" | custom-call | tf_op jit(solution)/shard_map/project/pallas_call | solution.py:274
  142.5 17.0 %all-to-all-start = ((f32[16,24,128]{2,1,0:T(8,128)}), f32[16,24,128]{2,1,0:T(8,128)S(1)}, u32[]{:S(2)}, u32[]{:S(2)}) async-start(f32[16,24,128]{2,1,0:T(8,128)} %get-tuple-element.7), calls=%async_computation | async-start | bytes 393216 | tf_op jit(solution)/shard_map/all_to_all | solution.py:413
  160.1 8.4 %all-to-all-done = f32[16,24,128]{2,1,0:T(8,128)S(1)} async-done(((f32[16,24,128]{2,1,0:T(8,128)}), f32[16,24,128]{2,1,0:T(8,128)S(1)}, u32[]{:S(2)}, u32[]{:S(2)}) %all-to-all-start) | async-done | bytes 196640 | tf_op jit(solution)/shard_map/all_to_all | solution.py:413
  168.5 1.6 divide_select_fusion
  (109 shorter events, 21.8 us)
Async XLA Ops:
  1.7 14.2 %collective-permute-start.15 = (bf16[64,2688]{1,0:T(8,128)(2,1)S(1)}, bf16[64,2688]{1,0:T(8,128)(2,1)}, u32[]{:S(2)}, u32[]{:S(2)}) collective-permute-start(bf16[64,2688]{1,0:T(8,128)(2,1)S(1)} %constant_dynamic-slice_fusion), channel_id=1, source_target_pairs={{0,4},{1,5},{2,6},{3,7},{4,8},{5,9},{6,10},{7,11},{8,12},{9,13},{1... | collective-permute-start | bytes 1032200 | tf_op jit(solution)/shard_map/ppermute | solution.py:46
  4.8 17.0 %collective-permute-start.23 = (bf16[64,2688]{1,0:T(8,128)(2,1)S(1)}, bf16[64,2688]{1,0:T(8,128)(2,1)}, u32[]{:S(2)}, u32[]{:S(2)}) collective-permute-start(bf16[64,2688]{1,0:T(8,128)(2,1)S(1)} %constant_dynamic-slice_fusion), channel_id=1, source_target_pairs={{0,12},{1,13},{2,14},{3,15},{4,0},{5,1},{6,2},{7,3},{8,4},{9,5},{1... | collective-permute-start | bytes 1032200 | tf_op jit(solution)/shard_map/ppermute | solution.py:46
  6.9 18.7 %collective-permute-start.11 = (bf16[64,2688]{1,0:T(8,128)(2,1)S(1)}, bf16[64,2688]{1,0:T(8,128)(2,1)}, u32[]{:S(2)}, u32[]{:S(2)}) collective-permute-start(bf16[64,2688]{1,0:T(8,128)(2,1)S(1)} %constant_dynamic-slice_fusion), channel_id=1, source_target_pairs={{0,2},{1,3},{2,0},{3,1},{4,6},{5,7},{6,4},{7,5},{8,10},{9,11},{10,... | collective-permute-start | bytes 1032200 | tf_op jit(solution)/shard_map/ppermute | solution.py:46
  8.6 42.4 %collective-permute-start.1 = (bf16[256,1024]{1,0:T(8,128)(2,1)}, bf16[256,1024]{1,0:T(8,128)(2,1)S(1)}, u32[]{:S(2)}, u32[]{:S(2)}) collective-permute-start(bf16[256,1024]{1,0:T(8,128)(2,1)} %refs_0_.2), channel_id=1, source_target_pairs={{0,4},{1,5},{2,6},{3,7},{4,8},{5,9},{6,10},{7,11},{8,12},{9,13},{1... | collective-permute-start | bytes 1572872 | tf_op jit(solution)/shard_map/ppermute | solution.py:46
  10.3 41.2 %collective-permute-start.6 = (bf16[256,1024]{1,0:T(8,128)(2,1)}, bf16[256,1024]{1,0:T(8,128)(2,1)S(1)}, u32[]{:S(2)}, u32[]{:S(2)}) collective-permute-start(bf16[256,1024]{1,0:T(8,128)(2,1)} %refs_6_.1), channel_id=1, source_target_pairs={{0,4},{1,5},{2,6},{3,7},{4,8},{5,9},{6,10},{7,11},{8,12},{9,13},{1... | collective-permute-start | bytes 1572872 | tf_op jit(solution)/shard_map/ppermute | solution.py:46
  15.9 37.1 %collective-permute-start = (bf16[256,1024]{1,0:T(8,128)(2,1)}, bf16[256,1024]{1,0:T(8,128)(2,1)S(1)}, u32[]{:S(2)}, u32[]{:S(2)}) collective-permute-start(bf16[256,1024]{1,0:T(8,128)(2,1)} %refs_0_.2), channel_id=1, source_target_pairs={{0,1},{2,3},{4,5},{6,7},{8,9},{10,11},{12,13},{14,15},{16,17},{18,... | collective-permute-start | bytes 1572872 | tf_op jit(solution)/shard_map/ppermute | solution.py:46
  21.8 27.6 %collective-permute-start.31 = (bf16[64,2688]{1,0:T(8,128)(2,1)S(1)}, bf16[64,2688]{1,0:T(8,128)(2,1)}, u32[]{:S(2)}, u32[]{:S(2)}) collective-permute-start(bf16[64,2688]{1,0:T(8,128)(2,1)S(1)} %constant_dynamic-slice_fusion), channel_id=1, source_target_pairs={{0,8},{1,9},{2,10},{3,11},{4,12},{5,13},{6,14},{7,15},{8,0},{9,1},... | collective-permute-start | bytes 1032200 | tf_op jit(solution)/shard_map/ppermute | solution.py:46
  25.6 27.9 %collective-permute-start.5 = (bf16[256,1024]{1,0:T(8,128)(2,1)}, bf16[256,1024]{1,0:T(8,128)(2,1)S(1)}, u32[]{:S(2)}, u32[]{:S(2)}) collective-permute-start(bf16[256,1024]{1,0:T(8,128)(2,1)} %refs_6_.1), channel_id=1, source_target_pairs={{0,1},{2,3},{4,5},{6,7},{8,9},{10,11},{12,13},{14,15},{16,17},{18,... | collective-permute-start | bytes 1572872 | tf_op jit(solution)/shard_map/ppermute | solution.py:46
  49.4 11.2 %collective-permute-start.19 = (bf16[64,2688]{1,0:T(8,128)(2,1)}, bf16[64,2688]{1,0:T(8,128)(2,1)}, u32[]{:S(2)}, u32[]{:S(2)}) collective-permute-start(bf16[64,2688]{1,0:T(8,128)(2,1)} %collective-permute-done.15.refs_6_), channel_id=1, source_target_pairs={{0,2},{1,3},{2,0},{3,1},{4,6},{5,7},{6,4},{7,5},{8,10},{9,11},{10,... | collective-permute-start | bytes 1032200 | tf_op jit(solution)/shard_map/ppermute | solution.py:46
  50.9 15.1 %collective-permute-start.27 = (bf16[64,2688]{1,0:T(8,128)(2,1)}, bf16[64,2688]{1,0:T(8,128)(2,1)}, u32[]{:S(2)}, u32[]{:S(2)}) collective-permute-start(bf16[64,2688]{1,0:T(8,128)(2,1)} %collective-permute-done.23.refs_14_), channel_id=1, source_target_pairs={{0,2},{1,3},{2,0},{3,1},{4,6},{5,7},{6,4},{7,5},{8,10},{9,11},{10,... | collective-permute-start | bytes 1032200 | tf_op jit(solution)/shard_map/ppermute | solution.py:46
  51.5 14.6 %collective-permute-start.16 = (bf16[64,2688]{1,0:T(8,128)(2,1)}, bf16[64,2688]{1,0:T(8,128)(2,1)}, u32[]{:S(2)}, u32[]{:S(2)}) collective-permute-start(bf16[64,2688]{1,0:T(8,128)(2,1)} %collective-permute-done.15.refs_6_), channel_id=1, source_target_pairs={{0,16},{16,0},{1,17},{17,1},{2,18},{18,2},{3,19},{19,3},{4,20},{20... | collective-permute-start | bytes 1032200 | tf_op jit(solution)/shard_map/ppermute | solution.py:333
  53.0 17.1 %collective-permute-start.24 = (bf16[64,2688]{1,0:T(8,128)(2,1)}, bf16[64,2688]{1,0:T(8,128)(2,1)}, u32[]{:S(2)}, u32[]{:S(2)}) collective-permute-start(bf16[64,2688]{1,0:T(8,128)(2,1)} %collective-permute-done.23.refs_14_), channel_id=1, source_target_pairs={{0,16},{16,0},{1,17},{17,1},{2,18},{18,2},{3,19},{19,3},{4,20},{20... | collective-permute-start | bytes 1032200 | tf_op jit(solution)/shard_map/ppermute | solution.py:333
  53.5 27.6 %collective-permute-start.10 = (bf16[128,2688]{1,0:T(8,128)(2,1)}, bf16[128,2688]{1,0:T(8,128)(2,1)S(1)}, u32[]{:S(2)}, u32[]{:S(2)}) collective-permute-start(bf16[128,2688]{1,0:T(8,128)(2,1)} %refs_0_.3), channel_id=1, source_target_pairs={{0,1},{1,0},{2,3},{3,2},{4,5},{5,4},{6,7},{7,6},{8,9},{9,8},{10,11... | collective-permute-start | bytes 2064392 | tf_op jit(solution)/shard_map/ppermute | solution.py:46
  60.7 14.2 %collective-permute-start.12 = (bf16[64,2688]{1,0:T(8,128)(2,1)}, bf16[64,2688]{1,0:T(8,128)(2,1)}, u32[]{:S(2)}, u32[]{:S(2)}) collective-permute-start(bf16[64,2688]{1,0:T(8,128)(2,1)} %collective-permute-done.11.refs_2_), channel_id=1, source_target_pairs={{0,16},{16,0},{1,17},{17,1},{2,18},{18,2},{3,19},{19,3},{4,20},{20... | collective-permute-start | bytes 1032200 | tf_op jit(solution)/shard_map/ppermute | solution.py:333
  66.1 10.3 %collective-permute-start.17 = (bf16[64,2688]{1,0:T(8,128)(2,1)}, bf16[64,2688]{1,0:T(8,128)(2,1)}, u32[]{:S(2)}, u32[]{:S(2)}) collective-permute-start(bf16[64,2688]{1,0:T(8,128)(2,1)} %collective-permute-done.15.refs_6_), channel_id=1, source_target_pairs={{0,1},{1,0},{2,3},{3,2},{4,5},{5,4},{6,7},{7,6},{8,9},{9,8},{10,11... | collective-permute-start | bytes 1032200 | tf_op jit(solution)/shard_map/ppermute | solution.py:46
  66.1 11.9 %collective-permute-start.25 = (bf16[64,2688]{1,0:T(8,128)(2,1)}, bf16[64,2688]{1,0:T(8,128)(2,1)}, u32[]{:S(2)}, u32[]{:S(2)}) collective-permute-start(bf16[64,2688]{1,0:T(8,128)(2,1)} %collective-permute-done.23.refs_14_), channel_id=1, source_target_pairs={{0,1},{1,0},{2,3},{3,2},{4,5},{5,4},{6,7},{7,6},{8,9},{9,8},{10,11... | collective-permute-start | bytes 1032200 | tf_op jit(solution)/shard_map/ppermute | solution.py:46
  76.4 11.1 %collective-permute-start.32 = (bf16[64,2688]{1,0:T(8,128)(2,1)}, bf16[64,2688]{1,0:T(8,128)(2,1)S(1)}, u32[]{:S(2)}, u32[]{:S(2)}) collective-permute-start(bf16[64,2688]{1,0:T(8,128)(2,1)} %collective-permute-done.31.refs_1_), channel_id=1, source_target_pairs={{0,16},{16,0},{1,17},{17,1},{2,18},{18,2},{3,19},{19,3},{4,20},{20... | collective-permute-start | bytes 1032200 | tf_op jit(solution)/shard_map/ppermute | solution.py:333
  78.0 17.0 %collective-permute-start.20 = (bf16[64,2688]{1,0:T(8,128)(2,1)}, bf16[64,2688]{1,0:T(8,128)(2,1)S(1)}, u32[]{:S(2)}, u32[]{:S(2)}) collective-permute-start(bf16[64,2688]{1,0:T(8,128)(2,1)} %collective-permute-done.19.refs_10_), channel_id=1, source_target_pairs={{0,16},{16,0},{1,17},{17,1},{2,18},{18,2},{3,19},{19,3},{4,20},{20... | collective-permute-start | bytes 1032200 | tf_op jit(solution)/shard_map/ppermute | solution.py:333
  78.5 20.2 %collective-permute-start.28 = (bf16[64,2688]{1,0:T(8,128)(2,1)}, bf16[64,2688]{1,0:T(8,128)(2,1)S(1)}, u32[]{:S(2)}, u32[]{:S(2)}) collective-permute-start(bf16[64,2688]{1,0:T(8,128)(2,1)} %collective-permute-done.27.refs_18_), channel_id=1, source_target_pairs={{0,16},{16,0},{1,17},{17,1},{2,18},{18,2},{3,19},{19,3},{4,20},{20... | collective-permute-start | bytes 1032200 | tf_op jit(solution)/shard_map/ppermute | solution.py:333
  81.1 17.5 %collective-permute-start.21 = (bf16[64,2688]{1,0:T(8,128)(2,1)}, bf16[64,2688]{1,0:T(8,128)(2,1)S(1)}, u32[]{:S(2)}, u32[]{:S(2)}) collective-permute-start(bf16[64,2688]{1,0:T(8,128)(2,1)} %collective-permute-done.19.refs_10_), channel_id=1, source_target_pairs={{0,1},{1,0},{2,3},{3,2},{4,5},{5,4},{6,7},{7,6},{8,9},{9,8},{10,11... | collective-permute-start | bytes 1032200 | tf_op jit(solution)/shard_map/ppermute | solution.py:46
  82.8 16.4 %collective-permute-start.29 = (bf16[64,2688]{1,0:T(8,128)(2,1)}, bf16[64,2688]{1,0:T(8,128)(2,1)S(1)}, u32[]{:S(2)}, u32[]{:S(2)}) collective-permute-start(bf16[64,2688]{1,0:T(8,128)(2,1)} %collective-permute-done.27.refs_18_), channel_id=1, source_target_pairs={{0,1},{1,0},{2,3},{3,2},{4,5},{5,4},{6,7},{7,6},{8,9},{9,8},{10,11... | collective-permute-start | bytes 1032200 | tf_op jit(solution)/shard_map/ppermute | solution.py:46
  87.6 17.1 %collective-permute-start.3 = (bf16[256,1024]{1,0:T(8,128)(2,1)S(1)}, bf16[256,1024]{1,0:T(8,128)(2,1)S(1)}, u32[]{:S(2)}, u32[]{:S(2)}) collective-permute-start(bf16[256,1024]{1,0:T(8,128)(2,1)S(1)} %broadcast_select_fusion.1), channel_id=1, source_target_pairs={{0,2},{1,3},{2,0},{3,1},{4,6},{5,7},{6,4},{7,5},{8,10},{9,11},{10,... | collective-permute-start | bytes 1572872 | tf_op jit(solution)/shard_map/ppermute | solution.py:46
  95.0 13.6 %collective-permute-start.8 = (bf16[256,1024]{1,0:T(8,128)(2,1)S(1)}, bf16[256,1024]{1,0:T(8,128)(2,1)S(1)}, u32[]{:S(2)}, u32[]{:S(2)}) collective-permute-start(bf16[256,1024]{1,0:T(8,128)(2,1)S(1)} %broadcast_select_fusion), channel_id=1, source_target_pairs={{0,2},{1,3},{2,0},{3,1},{4,6},{5,7},{6,4},{7,5},{8,10},{9,11},{10,... | collective-permute-start | bytes 1572872 | tf_op jit(solution)/shard_map/ppermute | solution.py:46
  100.5 10.4 %collective-permute-start.36 = (bf16[64,2688]{1,0:T(8,128)(2,1)}, bf16[64,2688]{1,0:T(8,128)(2,1)}, u32[]{:S(2)}, u32[]{:S(2)}) collective-permute-start(bf16[64,2688]{1,0:T(8,128)(2,1)} %collective-permute-done.35.refs_5_), channel_id=1, source_target_pairs={{0,16},{16,0},{1,17},{17,1},{2,18},{18,2},{3,19},{19,3},{4,20},{20... | collective-permute-start | bytes 1032200 | tf_op jit(solution)/shard_map/ppermute | solution.py:333
  102.1 11.5 %collective-permute-start.2 = (bf16[256,1024]{1,0:T(8,128)(2,1)S(1)}, bf16[256,1024]{1,0:T(8,128)(2,1)S(1)}, u32[]{:S(2)}, u32[]{:S(2)}) collective-permute-start(bf16[256,1024]{1,0:T(8,128)(2,1)S(1)} %collective-permute-done.1.refs_2_), channel_id=1, source_target_pairs={{1,0},{3,2},{5,4},{7,6},{9,8},{11,10},{13,12},{15,14},{17,16},{19,... | collective-permute-start | bytes 1572872 | tf_op jit(solution)/shard_map/ppermute | solution.py:46
  103.4 10.8 %collective-permute-start.7 = (bf16[256,1024]{1,0:T(8,128)(2,1)S(1)}, bf16[256,1024]{1,0:T(8,128)(2,1)}, u32[]{:S(2)}, u32[]{:S(2)}) collective-permute-start(bf16[256,1024]{1,0:T(8,128)(2,1)S(1)} %collective-permute-done.6.refs_8_), channel_id=1, source_target_pairs={{1,0},{3,2},{5,4},{7,6},{9,8},{11,10},{13,12},{15,14},{17,16},{19,... | collective-permute-start | bytes 1572872 | tf_op jit(solution)/shard_map/ppermute | solution.py:46
  104.7 10.0 %collective-permute-start.4 = (bf16[256,1024]{1,0:T(8,128)(2,1)S(1)}, bf16[256,1024]{1,0:T(8,128)(2,1)}, u32[]{:S(2)}, u32[]{:S(2)}) collective-permute-start(bf16[256,1024]{1,0:T(8,128)(2,1)S(1)} %collective-permute-done.3.refs_4_), channel_id=1, source_target_pairs={{0,1},{1,0},{2,3},{3,2},{4,5},{5,4},{6,7},{7,6},{8,9},{9,8},{10,11... | collective-permute-start | bytes 1572872 | tf_op jit(solution)/shard_map/ppermute | solution.py:46
  113.6 20.2 %collective-permute-start.33 = (bf16[64,2688]{1,0:T(8,128)(2,1)}, bf16[64,2688]{1,0:T(8,128)(2,1)S(1)}, u32[]{:S(2)}, u32[]{:S(2)}) collective-permute-start(bf16[64,2688]{1,0:T(8,128)(2,1)} %collective-permute-done.31.refs_1_), channel_id=1, source_target_pairs={{0,1},{1,0},{2,3},{3,2},{4,5},{5,4},{6,7},{7,6},{8,9},{9,8},{10,11... | collective-permute-start | bytes 1032200 | tf_op jit(solution)/shard_map/ppermute | solution.py:46
  114.2 19.6 %collective-permute-start.37 = (bf16[64,2688]{1,0:T(8,128)(2,1)}, bf16[64,2688]{1,0:T(8,128)(2,1)S(1)}, u32[]{:S(2)}, u32[]{:S(2)}) collective-permute-start(bf16[64,2688]{1,0:T(8,128)(2,1)} %collective-permute-done.35.refs_5_), channel_id=1, source_target_pairs={{0,1},{1,0},{2,3},{3,2},{4,5},{5,4},{6,7},{7,6},{8,9},{9,8},{10,11... | collective-permute-start | bytes 1032200 | tf_op jit(solution)/shard_map/ppermute | solution.py:46
  114.3 19.6 %collective-permute-start.34 = (bf16[64,2688]{1,0:T(8,128)(2,1)}, bf16[64,2688]{1,0:T(8,128)(2,1)}, u32[]{:S(2)}, u32[]{:S(2)}) collective-permute-start(bf16[64,2688]{1,0:T(8,128)(2,1)} %copy-done.9), channel_id=1, source_target_pairs={{0,1},{1,0},{2,3},{3,2},{4,5},{5,4},{6,7},{7,6},{8,9},{9,8},{10,11... | collective-permute-start | bytes 1032200 | tf_op jit(solution)/shard_map/ppermute | solution.py:46
  114.8 19.0 %collective-permute-start.38 = (bf16[64,2688]{1,0:T(8,128)(2,1)}, bf16[64,2688]{1,0:T(8,128)(2,1)}, u32[]{:S(2)}, u32[]{:S(2)}) collective-permute-start(bf16[64,2688]{1,0:T(8,128)(2,1)} %collective-permute-done.36.refs_6_), channel_id=1, source_target_pairs={{0,1},{1,0},{2,3},{3,2},{4,5},{5,4},{6,7},{7,6},{8,9},{9,8},{10,11... | collective-permute-start | bytes 1032200 | tf_op jit(solution)/shard_map/ppermute | solution.py:46
  142.5 26.0 %all-to-all-start = ((f32[16,24,128]{2,1,0:T(8,128)}), f32[16,24,128]{2,1,0:T(8,128)S(1)}, u32[]{:S(2)}, u32[]{:S(2)}) async-start(f32[16,24,128]{2,1,0:T(8,128)} %get-tuple-element.7), calls=%async_computation | async-start | bytes 393216 | tf_op jit(solution)/shard_map/all_to_all | solution.py:413
  (29 other events, 502.3 us)
where the time goes:
time: 171 us; the launch traced here: 170 us
  waiting for transfers between devices  78 us (46%)
  starting transfers between devices  56.1 us (33%)
  Pallas kernels  24.5 us (14%)
  other arithmetic  6.19 us (4%)
  local copies, waits for them, and re-layouts  3.75 us (2%)
    ppermute x32, waiting for transfers between devices, moved(): return lax.ppermute(block, 'seq', route)  45 us
    ppermute x32, starting transfers between devices, moved(): return lax.ppermute(block, 'seq', route)  30.5 us
    ppermute x7, waiting for transfers between devices, over_y(): return lax.ppermute(block, 'groups', [(0, 1), (1, 0)])  24.6 us
    all_to_all x1, starting transfers between devices, body(): arrived = lax.all_to_all(send, 'seq', 0, 0, tiled=True)  17 us
    pallas_call x1, Pallas kernels, project_early(): pl.pallas_call(kernel, in_specs=[smem, smem, whole] + [pl.BlockSpec(memor...  9.32 us
    ppermute x7, starting transfers between devices, over_y(): return lax.ppermute(block, 'groups', [(0, 1), (1, 0)])  8.61 us
    all_to_all x1, waiting for transfers between devices, body(): arrived = lax.all_to_all(send, 'seq', 0, 0, tiled=True)  8.38 us
    pallas_call x1, Pallas kernels, project(): pl.pallas_call(kernel, in_specs=[smem, smem, smem, whole, whole, whole] +...  7.86 us
  transfers between devices with their start and end apart: 40, of which 15 were waited for; matrix products, arithmetic and copies ran while one was open for 4% of the time, Pallas kernels for 10%

commit v1 on v0

v1 whole, which is shorter than its diff:
```python
import math

import jax
import jax.numpy as jnp
from jax import lax
from jax.experimental import pallas as pl
from jax.experimental.pallas import tpu as pltpu
from jax.sharding import PartitionSpec as P


HEAD_FEATURES = 128
WINDOW_SPAN = 1024
SLOTS = 2
LANES = 128
UNUSED = 2**30

query_scale = 168.0 ** (-0.5)
norm_eps = 1e-06


def chip_grid(mesh):
    devices = mesh.devices.reshape(mesh.shape["groups"], mesh.shape["seq"])
    where = [(*d.coords, d.core_on_chip) for d in devices[0]]
    xs = len({w[0] for w in where})
    zs = len({w[2] for w in where})
    if xs * zs * 2 != len(where):
        return None
    return zs, xs


def passed_along(block, axis, distance):
    devices = range(lax.axis_size(axis))
    route = [(i - distance, i) for i in devices if i - distance in devices]
    return lax.ppermute(block, axis, route)


def moved(block, grid, step):
    zs, xs = grid
    route = []
    for z in range(zs):
        for x in range(xs):
            for c in range(2):
                to = step(z, x, c)
                if to is not None:
                    route.append(((z * xs + x) * 2 + c, (to[0] * xs + to[1]) * 2 + to[2]))
    return lax.ppermute(block, "seq", route)


def last_start_at(pos, prev, s0, s1):
    last = jnp.maximum(prev, jnp.where(s0 <= pos, s0, 0))
    return jnp.maximum(last, jnp.where(s1 <= pos, s1, 0))


def attend(meta, queries, key_blocks, value_blocks, block_at, lower, upper, per_step):
    rows, width = queries.shape
    kv_width = key_blocks[0].shape[1]
    each = width // kv_width
    count = len(key_blocks)
    tall = each * rows
    to_exp2 = query_scale * math.log2(math.e)
    steps, skip = (upper - lower) // per_step, lower // per_step

    def kernel(meta, q_ref, *refs):
        k_refs, v_refs = refs[:count], refs[count : 2 * count]
        out_ref, bias, s_ref, m_ref, l_ref, acc = refs[2 * count :]
        first = meta[0] * rows
        prev, s0, s1 = meta[1], meta[2], meta[3]
        lowest = jnp.maximum(last_start_at(first, prev, s0, s1), first - WINDOW_SPAN + 1)
        places = []
        for b in range(count):
            index, valid = block_at(b, meta[0])
            start = index * rows
            places.append((start, valid & (index >= 0) & (start + rows > lowest)))

        @pl.when(pl.program_id(0) == 0)
        def _():
            for b, (start, need) in enumerate(places):

                @pl.when(need)
                def _():
                    q_pos = first + lax.broadcasted_iota(jnp.int32, (rows, rows), 0)
                    k_pos = start + lax.broadcasted_iota(jnp.int32, (rows, rows), 1)
                    low = last_start_at(q_pos, prev, s0, s1)
                    low = jnp.maximum(low, q_pos - WINDOW_SPAN + 1)
                    visible = (k_pos >= low) & (k_pos <= q_pos)
                    bias[b] = jnp.where(visible, 0.0, -jnp.inf)

        m_ref[...] = jnp.full(m_ref.shape, -jnp.inf, jnp.float32)
        l_ref[...] = jnp.zeros(l_ref.shape, jnp.float32)
        acc[...] = jnp.zeros(acc.shape, jnp.float32)

        def lanes(block):
            return [block[:, t : t + LANES] for t in range(0, rows, LANES)]

        for b, (start, need) in enumerate(places):

            @pl.when(need)
            def _():
                for g in range(per_step):
                    k = k_refs[b][:, g * HEAD_FEATURES : (g + 1) * HEAD_FEATURES]
                    for r in range(each):
                        at = (g * each + r) * HEAD_FEATURES
                        s = lax.dot_general(
                            q_ref[:, at : at + HEAD_FEATURES],
                            k,
                            (((1,), (1,)), ((), ())),
                            preferred_element_type=jnp.float32,
                        )
                        s = s + bias[b]
                        s_ref[b, g, r * rows : (r + 1) * rows] = s
                        top = m_ref[g, r * rows : (r + 1) * rows]
                        for part in lanes(s):
                            top = jnp.maximum(top, part)
                        m_ref[g, r * rows : (r + 1) * rows] = top

        for g in range(per_step):
            peak = jnp.max(m_ref[g], axis=1, keepdims=True)
            m_ref[g] = jnp.broadcast_to(peak, (tall, LANES))

        for b, (start, need) in enumerate(places):

            @pl.when(need)
            def _():
                for g in range(per_step):
                    peak = m_ref[g]
                    parts = [jnp.exp2((part - peak) * to_exp2) for part in lanes(s_ref[b, g])]
                    l_ref[g] += sum(parts[1:], parts[0])
                    p = jnp.concatenate([part.astype(jnp.bfloat16) for part in parts], axis=1)
                    acc[g] += jnp.dot(
                        p,
                        v_refs[b][:, g * HEAD_FEATURES : (g + 1) * HEAD_FEATURES],
                        preferred_element_type=jnp.float32,
                    )

        for g in range(per_step):
            totals = jnp.sum(l_ref[g], axis=1, keepdims=True)
            result = (acc[g] / totals).astype(jnp.bfloat16)
            for r in range(each):
                at = (g * each + r) * HEAD_FEATURES
                out_ref[:, at : at + HEAD_FEATURES] = result[r * rows : (r + 1) * rows]

    wide = per_step * each * HEAD_FEATURES
    q_spec = pl.BlockSpec((rows, wide), lambda g, meta: (0, g + skip))
    kv_spec = pl.BlockSpec((rows, per_step * HEAD_FEATURES), lambda g, meta: (0, g + skip))
    out_spec = pl.BlockSpec((rows, wide), lambda g, meta: (0, g))
    return pl.pallas_call(
        kernel,
        grid_spec=pltpu.PrefetchScalarGridSpec(
            num_scalar_prefetch=1,
            grid=(steps,),
            in_specs=[q_spec] + [kv_spec] * (2 * count),
            out_specs=out_spec,
            scratch_shapes=[
                pltpu.VMEM((count, rows, rows), jnp.float32),
                pltpu.VMEM((count, per_step, tall, rows), jnp.float32),
                pltpu.VMEM((per_step, tall, LANES), jnp.float32),
                pltpu.VMEM((per_step, tall, LANES), jnp.float32),
                pltpu.VMEM((per_step, tall, HEAD_FEATURES), jnp.float32),
            ],
        ),
        out_shape=jax.ShapeDtypeStruct((rows, steps * wide), jnp.bfloat16),
        name="attend",
    )(meta, queries, *key_blocks, *value_blocks)


def gathered(refs, w_ref, offs, sems):
    copies = []
    for i, ref in enumerate(refs):
        tall = ref.shape[0]
        at = pl.multiple_of(offs[i], math.gcd(tall, 16))
        copies.append(pltpu.make_async_copy(ref, w_ref.at[pl.ds(at, tall)], sems.at[i]))
    return copies


def joined(parts, whole_ref):
    at = 0
    for ref in parts:
        whole_ref[:, at : at + ref.shape[1]] = ref[...]
        at += ref.shape[1]


def column_spans(columns):
    return [(at, min(512, columns - at)) for at in range(0, columns, 512)]


def project(meta, chunk_at, attended, residual, post_scale, pieces, offsets, slots, seq_size):
    rows = attended[0].shape[0]
    width = sum(a.shape[1] for a in attended)
    columns = residual.shape[1]
    count = len(pieces)
    chunks = chunk_at.shape[0]
    chunk = width // chunks
    spans = column_spans(columns)
    lines = -(-columns // (8 * LANES)) * 8

    def kernel(meta, chunk_at, offs, post_ref, *refs):
        att_parts, refs = refs[: len(attended)], refs[len(attended) :]
        piece_refs, res_hbm = refs[:count], refs[count]
        hidden_ref, sums_ref, send_ref, w_ref, proj, att_ref, res_ref, row_ref, sems, res_sem = refs[
            count + 1 :
        ]
        copies = gathered(piece_refs, w_ref, offs, sems)
        for i in range(chunks):
            for copy, slot in zip(copies, slots):
                if slot == i:
                    copy.start()
        res_copy = pltpu.make_async_copy(res_hbm, res_ref, res_sem)
        res_copy.start()
        joined(att_parts, att_ref)
        first = meta[0] * rows
        prev, s0, s1 = meta[1], meta[2], meta[3]
        pos = first + lax.broadcasted_iota(jnp.int32, (rows, LANES), 0)
        last = last_start_at(pos, prev, s0, s1)
        masks = [m.astype(jnp.float32) for m in (last == s0, last == s1, last < first)]
        square = jnp.zeros((rows, LANES), jnp.float32)
        for i in range(chunks):
            for copy, slot in zip(copies, slots):
                if slot == i:
                    copy.wait()
            att = att_ref[:, pl.ds(pl.multiple_of(chunk_at[i] * chunk, LANES), chunk)]
            for at, split in spans:
                part = jnp.dot(
                    att,
                    w_ref[i * chunk : (i + 1) * chunk, at : at + split],
                    preferred_element_type=jnp.float32,
                )
                if i > 0:
                    part = part + proj[:, at : at + split]
                proj[:, at : at + split] = part
                if i == chunks - 1:
                    for t in range(0, split, LANES):
                        square = square + part[:, t : t + LANES] * part[:, t : t + LANES]
        total = jnp.sum(square, axis=1, keepdims=True)
        norm = jnp.broadcast_to(lax.rsqrt(total * (1.0 / columns) + norm_eps), (rows, LANES))
        owner = prev // rows
        res_copy.wait()
        send_ref[...] = jnp.zeros(send_ref.shape, send_ref.dtype)
        row_ref[...] = jnp.zeros(row_ref.shape, jnp.float32)
        for at in range(0, columns, LANES):
            updated = res_ref[:, at : at + LANES].astype(jnp.float32) + (
                proj[:, at : at + LANES] * norm * post_ref[:, at : at + LANES]
            )
            hidden_ref[:, at : at + LANES] = updated.astype(jnp.bfloat16)
            sums = [jnp.sum(updated * m, axis=0, keepdims=True) for m in masks]
            for slot in range(SLOTS):
                sums_ref[slot : slot + 1, at : at + LANES] = sums[slot]
            row_ref[at // LANES : at // LANES + 1, :] = sums[SLOTS]
        send_ref[owner] = row_ref[...].astype(send_ref.dtype)

    whole = pl.BlockSpec(memory_space=pltpu.MemorySpace.VMEM)
    smem = pl.BlockSpec(memory_space=pltpu.MemorySpace.SMEM)
    return pl.pallas_call(
        kernel,
        in_specs=[smem, smem, smem, whole]
        + [whole] * len(attended)
        + [pl.BlockSpec(memory_space=pl.ANY)] * (count + 1),
        out_specs=(whole, whole, whole),
        out_shape=(
            jax.ShapeDtypeStruct((rows, columns), jnp.bfloat16),
            jax.ShapeDtypeStruct((SLOTS, columns), jnp.float32),
            jax.ShapeDtypeStruct((seq_size, lines, LANES), jnp.bfloat16),
        ),
        scratch_shapes=[
            pltpu.VMEM((width, columns), jnp.bfloat16),
            pltpu.VMEM((rows, columns), jnp.float32),
            pltpu.VMEM((rows, width), jnp.bfloat16),
            pltpu.VMEM((rows, columns), jnp.bfloat16),
            pltpu.VMEM((lines, LANES), jnp.float32),
            pltpu.SemaphoreType.DMA((count,)),
            pltpu.SemaphoreType.DMA,
        ],
        name="project",
    )(meta, chunk_at, offsets, post_scale[None, :], *attended, *pieces, residual)


def by_links(grid, groups, tok_rows, part_rows):
    return grid == (4, 2) and groups == 2 and WINDOW_SPAN == 4 * tok_rows and part_rows % 32 == 0


def body(grid, queries, keys, values, residual, out_weight, post_scale, doc_starts):
    seq_size = lax.axis_size("seq")
    my_index = lax.axis_index("seq")
    tok_rows = queries.shape[0]
    halo_blocks = WINDOW_SPAN // tok_rows
    part_rows = out_weight.shape[0]
    kv_heads = keys.shape[1] // HEAD_FEATURES

    slot_count = doc_starts.shape[0]
    slot_ids = jnp.arange(slot_count, dtype=jnp.int32)
    live_slot = doc_starts < (slot_ids // SLOTS + 1) * tok_rows
    first = my_index * tok_rows
    my_starts = lax.dynamic_slice_in_dim(doc_starts, my_index * SLOTS, SLOTS)
    my_live = my_starts < first + tok_rows
    prev = jnp.max(jnp.where(live_slot & (doc_starts < first), doc_starts, 0))
    shown = jnp.where(my_live, my_starts, UNUSED)
    meta = jnp.concatenate([my_index[None], prev[None], shown]).astype(jnp.int32)

    if by_links(grid, lax.axis_size("groups"), tok_rows, part_rows):
        zs, xs = grid
        half_rows = part_rows // 2
        z, x, c = my_index // 4, my_index // 2 % 2, my_index % 2
        y = lax.axis_index("groups")

        def turned(k):
            return lambda block: moved(block, grid, lambda z, x, c: ((z + k) % zs, x, c))

        def over_x(block):
            return moved(block, grid, lambda z, x, c: (z, 1 - x, c))

        def over_c(block):
            return moved(block, grid, lambda z, x, c: (z, x, 1 - c))

        def over_y(block):
            return lax.ppermute(block, "groups", [(0, 1), (1, 0)])

        def up(block):
            return moved(block, grid, lambda z, x, c: (z + 1, x, c) if z + 1 < zs else None)

        def right(block):
            return moved(block, grid, lambda z, x, c: (z, x, 1) if c == 0 else None)

        def left(block):
            return moved(block, grid, lambda z, x, c: (z, x, 0) if c == 1 else None)

        own = lax.dynamic_slice_in_dim(out_weight, y * half_rows, half_rows)
        pieces, offsets, slots = [], [], []

        def place(slot, piece, x, c, half):
            pieces.append(piece)
            offsets.append((slot * xs * 2 + x * 2 + c) * part_rows + half * half_rows)
            slots.append(slot)

        def place_all(slot, piece, x):
            other = over_y(piece)
            place(slot, piece, x, c, y)
            place(slot, other, x, c, 1 - y)
            place(slot, over_c(piece), x, 1 - c, y)
            place(slot, over_c(other), x, 1 - c, 1 - y)

        place(0, out_weight, x, c, 0)
        place(0, over_c(out_weight), x, 1 - c, 0)
        place_all(0, over_x(own), 1 - x)
        nearest = turned(1)(own)
        for slot, k in ((1, 1), (2, 3), (3, 2)):
            ring = nearest
            if k == 2:
                ring = turned(1)(nearest)
            if k == 3:
                ring = turned(3)(own)
            place_all(slot, ring, x)
            place_all(slot, over_x(ring), 1 - x)
        chunk_at = jnp.stack([z, (z - 1) % zs, (z - 3) % zs, (z - 2) % zs]).astype(jnp.int32)
        offsets = jnp.stack([jnp.asarray(o, jnp.int32) for o in offsets])

        groups = []
        for mine in (keys, values):
            below = up(mine)
            onward = jnp.where(x == 0, mine, below)
            aside = over_x(onward)
            groups.append([mine, right(mine), below, left(below), aside, over_c(aside)])
        key_blocks, value_blocks = groups

        def block_at(b, index):
            chip, core = index // 2, index % 2
            back = (0, 0, 2, 2, 1, 1)[b]
            place = (chip - back) * 2 + (core if b % 2 == 0 else 1 - core)
            valid = True
            if b == 1:
                valid = core == 1
            if b == 3:
                valid = core == 0
            return place, (place <= index) & valid

        attended = []
        half = kv_heads // 2
        for lower in (0, half):
            attended.append(
                attend(meta, queries, key_blocks, value_blocks, block_at, lower, lower + half, half)
            )
    else:
        pieces = [lax.all_gather(out_weight, "seq", axis=0, tiled=True)]
        offsets = jnp.zeros((1,), jnp.int32)
        chunk_at, slots = offsets, [0]
        key_blocks, value_blocks = [keys], [values]
        for distance in range(1, halo_blocks + 1):
            key_blocks.append(passed_along(keys, "seq", distance))
            value_blocks.append(passed_along(values, "seq", distance))

        def block_at(b, index):
            return index - b, index >= b

        attended = [
            attend(
                meta, queries, key_blocks, value_blocks, block_at, 0, kv_heads, math.gcd(kv_heads, 4)
            )
        ]

    hidden, slot_sums, send = project(
        meta, chunk_at, attended, residual, post_scale, pieces, offsets, slots, seq_size
    )
    arrived = lax.all_to_all(send, "seq", 0, 0, tiled=True)
    carried_sum = jnp.sum(arrived.astype(jnp.float32), axis=0).reshape(-1)[: residual.shape[1]]
    last_live = jnp.sum(my_live.astype(jnp.int32)) - 1
    tail_pick = (jnp.arange(SLOTS, dtype=jnp.int32) == last_live).astype(jnp.float32)
    doc_sums = slot_sums + tail_pick[:, None] * carried_sum[None, :]
    total_tokens = tok_rows * seq_size
    later_starts = live_slot[None, :] & (doc_starts[None, :] > my_starts[:, None])
    following = jnp.min(jnp.where(later_starts, doc_starts[None, :], total_tokens), axis=1)
    doc_length = jnp.maximum(following - my_starts, 1).astype(jnp.float32)
    pooled = jnp.where(my_live[:, None], doc_sums / doc_length[:, None], 0.0)
    return (hidden, pooled)


def solution(mesh):
    grid = chip_grid(mesh)
    placed = (
        P(("groups", "seq"), None),
        P(("groups", "seq"), None),
        P(("groups", "seq"), None),
        P(("groups", "seq"), None),
        P("seq", None),
        P(),
        P("groups"),
    )

    def whole(*args):
        return body(grid, *args)

    step = jax.shard_map(
        whole,
        mesh=mesh,
        in_specs=placed,
        out_specs=(P(("groups", "seq"), None), P(("groups", "seq"), None)),
        check_vma=False,
    )

    def run(queries, keys, values, residual, out_weight, post_scale, doc_starts):
        args = (queries, keys, values, residual, out_weight, post_scale, doc_starts)
        return step(*args)

    return run
```

time: 171 us -> 162 us (0.947)
  starting transfers between devices: 56.1 us -> 48.1 us
  waiting for transfers between devices: 78 us -> 82.8 us
  Pallas kernels: 24.5 us -> 20.3 us
    ppermute x7, waiting for transfers between devices: 24.6 us -> 33.2 us  [over_y(): return lax.ppermute(block, 'groups', [(0, 1), (1, 0)])]
    pallas_call x2 -> x1, Pallas kernels: 17.2 us -> 9.38 us  [project(): pl.pallas_call(kernel, in_specs=[smem, smem, smem, whole] + [whole] * len...]
    all_to_all x1, starting transfers between devices: 17 us -> 12.9 us  [body(): arrived = lax.all_to_all(send, 'seq', 0, 0, tiled=True)]
    pallas_call x1 -> x2, Pallas kernels: 7.3 us -> 10.9 us  [attend(): pl.pallas_call(kernel, grid_spec=pltpu.PrefetchScalarGridSpec(num_scalar_...]
    ppermute x32, starting transfers between devices: 30.5 us -> 27.2 us  [moved(): return lax.ppermute(block, 'seq', route)]
    ppermute x32, waiting for transfers between devices: 45 us -> 42.9 us  [moved(): return lax.ppermute(block, 'seq', route)]
  transfers between devices with their start and end apart: 40 -> 40, of which waited for: 15 -> 18; matrix products, arithmetic and copies ran while one was open for 4% -> 3% of each run, Pallas kernels for 10% -> 7%
where the time goes in v1:
time: 162 us
  waiting for transfers between devices  82.8 us (51%)
  starting transfers between devices  48.1 us (30%)
  Pallas kernels  20.3 us (13%)
  other arithmetic  5.49 us (3%)
  local copies, waits for them, and re-layouts  3.34 us (2%)
  between operations  1.66 us (1%)
    ppermute x32, waiting for transfers between devices, moved(): return lax.ppermute(block, 'seq', route)  42.9 us
    ppermute x7, waiting for transfers between devices, over_y(): return lax.ppermute(block, 'groups', [(0, 1), (1, 0)])  33.2 us
    ppermute x32, starting transfers between devices, moved(): return lax.ppermute(block, 'seq', route)  27.2 us
    all_to_all x1, starting transfers between devices, body(): arrived = lax.all_to_all(send, 'seq', 0, 0, tiled=True)  12.9 us
    pallas_call x2, Pallas kernels, attend(): pl.pallas_call(kernel, grid_spec=pltpu.PrefetchScalarGridSpec(num_scalar_...  10.9 us
    pallas_call x1, Pallas kernels, project(): pl.pallas_call(kernel, in_specs=[smem, smem, smem, whole] + [whole] * len...  9.38 us
    ppermute x7, starting transfers between devices, over_y(): return lax.ppermute(block, 'groups', [(0, 1), (1, 0)])  7.98 us
    all_to_all x1, waiting for transfers between devices, body(): arrived = lax.all_to_all(send, 'seq', 0, 0, tiled=True)  6.74 us
  transfers between devices with their start and end apart: 40, of which 18 were waited for; matrix products, arithmetic and copies ran while one was open for 3% of the time, Pallas kernels for 7%

profile of v1, /device:TPU:0, one launch (start us, length us, event | category | flops | bytes accessed | tf_op | source)
XLA Modules:
  0.0 161.7 jit_solution(11407079192975985477)
XLA Ops:
  1.7 3.1 %collective-permute-start.15 = (bf16[64,2688]{1,0:T(8,128)(2,1)S(1)}, bf16[64,2688]{1,0:T(8,128)(2,1)S(1)}, u32[]{:S(2)}, u32[]{:S(2)}) collective-permute-start(bf16[64,2688]{1,0:T(8,128)(2,1)S(1)} %constant_dynamic-slice_fusion), channel_id=1, source_target_pairs={{0,4},{1,5},{2,6},{3,7},{4,8},{5,9},{6,10},{7,11},{8,12},{9,13},{1... | collective-permute-start | bytes 1032200 | tf_op jit(solution)/shard_map/ppermute | solution.py:46
  4.8 2.1 %collective-permute-start.23 = (bf16[64,2688]{1,0:T(8,128)(2,1)S(1)}, bf16[64,2688]{1,0:T(8,128)(2,1)}, u32[]{:S(2)}, u32[]{:S(2)}) collective-permute-start(bf16[64,2688]{1,0:T(8,128)(2,1)S(1)} %constant_dynamic-slice_fusion), channel_id=1, source_target_pairs={{0,12},{1,13},{2,14},{3,15},{4,0},{5,1},{6,2},{7,3},{8,4},{9,5},{1... | collective-permute-start | bytes 1032200 | tf_op jit(solution)/shard_map/ppermute | solution.py:46
  6.9 1.9 %collective-permute-start.1 = (bf16[256,1024]{1,0:T(8,128)(2,1)}, bf16[256,1024]{1,0:T(8,128)(2,1)S(1)}, u32[]{:S(2)}, u32[]{:S(2)}) collective-permute-start(bf16[256,1024]{1,0:T(8,128)(2,1)} %refs_0_.3), channel_id=1, source_target_pairs={{0,4},{1,5},{2,6},{3,7},{4,8},{5,9},{6,10},{7,11},{8,12},{9,13},{1... | collective-permute-start | bytes 1572872 | tf_op jit(solution)/shard_map/ppermute | solution.py:46
  8.8 3.5 %collective-permute-start.6 = (bf16[256,1024]{1,0:T(8,128)(2,1)}, bf16[256,1024]{1,0:T(8,128)(2,1)S(1)}, u32[]{:S(2)}, u32[]{:S(2)}) collective-permute-start(bf16[256,1024]{1,0:T(8,128)(2,1)} %refs_6_.3), channel_id=1, source_target_pairs={{0,4},{1,5},{2,6},{3,7},{4,8},{5,9},{6,10},{7,11},{8,12},{9,13},{1... | collective-permute-start | bytes 1572872 | tf_op jit(solution)/shard_map/ppermute | solution.py:46
  13.6 2.2 %collective-permute-done.15.refs_8_ = bf16[64,2688]{1,0:T(8,128)(2,1)S(1)} collective-permute-done((bf16[64,2688]{1,0:T(8,128)(2,1)S(1)}, bf16[64,2688]{1,0:T(8,128)(2,1)S(1)}, u32[]{:S(2)}, u32[]{:S(2)}) %collective-permute-start.15) | collective-permute-done | bytes 344096 | tf_op jit(solution)/shard_map/ppermute | solution.py:46
  17.1 4.7 %collective-permute-done.23.refs_16_ = bf16[64,2688]{1,0:T(8,128)(2,1)} collective-permute-done((bf16[64,2688]{1,0:T(8,128)(2,1)S(1)}, bf16[64,2688]{1,0:T(8,128)(2,1)}, u32[]{:S(2)}, u32[]{:S(2)}) %collective-permute-start.23) | collective-permute-done | bytes 344096 | tf_op jit(solution)/shard_map/ppermute | solution.py:46
  21.8 1.5 collective-permute-start.11
  23.3 8.0 %collective-permute-done.11.refs_4_ = bf16[64,2688]{1,0:T(8,128)(2,1)} collective-permute-done((bf16[64,2688]{1,0:T(8,128)(2,1)S(1)}, bf16[64,2688]{1,0:T(8,128)(2,1)}, u32[]{:S(2)}, u32[]{:S(2)}) %collective-permute-start.11) | collective-permute-done | bytes 344096 | tf_op jit(solution)/shard_map/ppermute | solution.py:46
  31.3 1.7 %collective-permute-start.31 = (bf16[64,2688]{1,0:T(8,128)(2,1)S(1)}, bf16[64,2688]{1,0:T(8,128)(2,1)}, u32[]{:S(2)}, u32[]{:S(2)}) collective-permute-start(bf16[64,2688]{1,0:T(8,128)(2,1)S(1)} %collective-permute-done.15.refs_8_), channel_id=1, source_target_pairs={{0,4},{1,5},{2,6},{3,7},{4,8},{5,9},{6,10},{7,11},{8,12},{9,13},{1... | collective-permute-start | bytes 1032200 | tf_op jit(solution)/shard_map/ppermute | solution.py:46
  33.0 1.5 collective-permute-start.19
  34.5 8.7 %collective-permute-done.6.refs_8_ = bf16[256,1024]{1,0:T(8,128)(2,1)S(1)} collective-permute-done((bf16[256,1024]{1,0:T(8,128)(2,1)}, bf16[256,1024]{1,0:T(8,128)(2,1)S(1)}, u32[]{:S(2)}, u32[]{:S(2)}) %collective-permute-start.6) | collective-permute-done | bytes 524320 | tf_op jit(solution)/shard_map/ppermute | solution.py:46
  44.8 1.5 collective-permute-start.16
  46.8 2.6 %collective-permute-done.31.refs_24_ = bf16[64,2688]{1,0:T(8,128)(2,1)} collective-permute-done((bf16[64,2688]{1,0:T(8,128)(2,1)S(1)}, bf16[64,2688]{1,0:T(8,128)(2,1)}, u32[]{:S(2)}, u32[]{:S(2)}) %collective-permute-start.31) | collective-permute-done | bytes 344096 | tf_op jit(solution)/shard_map/ppermute | solution.py:46
  51.3 1.5 collective-permute-start.12
  52.8 2.9 %collective-permute-done.16.refs_9_ = bf16[64,2688]{1,0:T(8,128)(2,1)S(1)} collective-permute-done((bf16[64,2688]{1,0:T(8,128)(2,1)S(1)}, bf16[64,2688]{1,0:T(8,128)(2,1)S(1)}, u32[]{:S(2)}, u32[]{:S(2)}) %collective-permute-start.16) | collective-permute-done | bytes 344096 | tf_op jit(solution)/shard_map/ppermute | solution.py:314
  55.7 7.4 %collective-permute-done.24.refs_17_ = bf16[64,2688]{1,0:T(8,128)(2,1)S(1)} collective-permute-done((bf16[64,2688]{1,0:T(8,128)(2,1)}, bf16[64,2688]{1,0:T(8,128)(2,1)S(1)}, u32[]{:S(2)}, u32[]{:S(2)}) %collective-permute-start.24) | collective-permute-done | bytes 344096 | tf_op jit(solution)/shard_map/ppermute | solution.py:314
  63.7 3.4 %collective-permute-done.12.refs_5_ = bf16[64,2688]{1,0:T(8,128)(2,1)} collective-permute-done((bf16[64,2688]{1,0:T(8,128)(2,1)}, bf16[64,2688]{1,0:T(8,128)(2,1)}, u32[]{:S(2)}, u32[]{:S(2)}) %collective-permute-start.12) | collective-permute-done | bytes 344096 | tf_op jit(solution)/shard_map/ppermute | solution.py:314
  67.2 1.5 collective-permute-start.32
  70.7 3.2 %collective-permute-done.35.refs_28_ = bf16[64,2688]{1,0:T(8,128)(2,1)} collective-permute-done((bf16[64,2688]{1,0:T(8,128)(2,1)}, bf16[64,2688]{1,0:T(8,128)(2,1)}, u32[]{:S(2)}, u32[]{:S(2)}) %collective-permute-start.35) | collective-permute-done | bytes 344096 | tf_op jit(solution)/shard_map/ppermute | solution.py:46
  73.9 1.5 collective-permute-start.28
  75.5 1.8 %collective-permute-done.32.refs_25_ = bf16[64,2688]{1,0:T(8,128)(2,1)} collective-permute-done((bf16[64,2688]{1,0:T(8,128)(2,1)}, bf16[64,2688]{1,0:T(8,128)(2,1)}, u32[]{:S(2)}, u32[]{:S(2)}) %collective-permute-start.32) | collective-permute-done | bytes 344096 | tf_op jit(solution)/shard_map/ppermute | solution.py:314
  77.4 7.3 %collective-permute-done.20.refs_13_ = bf16[64,2688]{1,0:T(8,128)(2,1)} collective-permute-done((bf16[64,2688]{1,0:T(8,128)(2,1)}, bf16[64,2688]{1,0:T(8,128)(2,1)}, u32[]{:S(2)}, u32[]{:S(2)}) %collective-permute-start.20) | collective-permute-done | bytes 344096 | tf_op jit(solution)/shard_map/ppermute | solution.py:314
  84.7 1.5 collective-permute-start.3
  86.7 2.8 %collective-permute-done.28.refs_21_ = bf16[64,2688]{1,0:T(8,128)(2,1)} collective-permute-done((bf16[64,2688]{1,0:T(8,128)(2,1)S(1)}, bf16[64,2688]{1,0:T(8,128)(2,1)}, u32[]{:S(2)}, u32[]{:S(2)}) %collective-permute-start.28) | collective-permute-done | bytes 344096 | tf_op jit(solution)/shard_map/ppermute | solution.py:314
  93.9 5.2 %collective-permute-done.3.refs_4_ = bf16[256,1024]{1,0:T(8,128)(2,1)S(1)} collective-permute-done((bf16[256,1024]{1,0:T(8,128)(2,1)S(1)}, bf16[256,1024]{1,0:T(8,128)(2,1)S(1)}, u32[]{:S(2)}, u32[]{:S(2)}) %collective-permute-start.3) | collective-permute-done | bytes 524320 | tf_op jit(solution)/shard_map/ppermute | solution.py:46
  99.1 5.6 %collective-permute-done.8.refs_10_ = bf16[256,1024]{1,0:T(8,128)(2,1)S(1)} collective-permute-done((bf16[256,1024]{1,0:T(8,128)(2,1)S(1)}, bf16[256,1024]{1,0:T(8,128)(2,1)S(1)}, u32[]{:S(2)}, u32[]{:S(2)}) %collective-permute-start.8) | collective-permute-done | bytes 524320 | tf_op jit(solution)/shard_map/ppermute | solution.py:46
  107.9 7.6 %collective-permute-done.36.refs_29_ = bf16[64,2688]{1,0:T(8,128)(2,1)S(1)} collective-permute-done((bf16[64,2688]{1,0:T(8,128)(2,1)}, bf16[64,2688]{1,0:T(8,128)(2,1)S(1)}, u32[]{:S(2)}, u32[]{:S(2)}) %collective-permute-start.36) | collective-permute-done | bytes 344096 | tf_op jit(solution)/shard_map/ppermute | solution.py:314
  118.7 5.4 %attend.3.refs_1_ = bf16[256,1024]{1,0:T(8,128)(2,1)} custom-call(s32[4]{0:T(128)} %get-tuple-element.15.meta, bf16[256,2048]{1,0:T(8,128)(2,1)} %q_ref.3, bf16[256,1024]{1,0:T(8,128)(2,1)} %refs_0_.3, bf16[256,1024]{1,0:T(8,128)(2,1)} %copy-done.3, bf16[256,1024]{1,0:T(8,128)(2,1)} %copy-done.1, bf16[256,1024]{1,0:T(8,128)(2,1)} %copy-done.7, ...), custom_call_target="tpu_custom_call" | custom-call | tf_op jit(solution)/shard_map/attend/pallas_call | solution.py:146
  124.1 5.5 %attend.2.refs_0_ = bf16[256,1024]{1,0:T(8,128)(2,1)} custom-call(s32[4]{0:T(128)} %get-tuple-element.15.meta, bf16[256,2048]{1,0:T(8,128)(2,1)} %q_ref.3, bf16[256,1024]{1,0:T(8,128)(2,1)} %refs_0_.3, bf16[256,1024]{1,0:T(8,128)(2,1)} %copy-done.3, bf16[256,1024]{1,0:T(8,128)(2,1)} %copy-done.1, bf16[256,1024]{1,0:T(8,128)(2,1)} %copy-done.7, ...), custom_call_target="tpu_custom_call" | custom-call | tf_op jit(solution)/shard_map/attend/pallas_call | solution.py:146
  130.6 9.4 %project.1 = (bf16[256,2688]{1,0:T(8,128)(2,1)}, f32[2,2688]{1,0:T(2,128)}, bf16[16,24,128]{2,1,0:T(8,128)(2,1)}) custom-call(s32[4]{0:T(128)} %get-tuple-element.15.meta, s32[4]{0:T(128)} %get-tuple-element.16.chunk_at, s32[30]{0:T(128)} %stack.143.offs, f32[1,2688]{1,0:T(1,128)} %broadcast_in_dim.48.post_ref, bf16[256,1024]{1,0:T(8,128)(2,1)} %attend.2.refs_0_, ...), custom_call_target="tpu_custom_call" | custom-call | tf_op jit(solution)/shard_map/project/pallas_call | solution.py:252
  140.0 12.9 %all-to-all-start = ((bf16[16,24,128]{2,1,0:T(8,128)(2,1)}), bf16[16,24,128]{2,1,0:T(8,128)(2,1)S(1)}, u32[]{:S(2)}, u32[]{:S(2)}) async-start(bf16[16,24,128]{2,1,0:T(8,128)(2,1)} %get-tuple-element.7), calls=%async_computation | async-start | bytes 196608 | tf_op jit(solution)/shard_map/all_to_all | solution.py:401
  153.5 6.7 %all-to-all-done = bf16[16,24,128]{2,1,0:T(8,128)(2,1)S(1)} async-done(((bf16[16,24,128]{2,1,0:T(8,128)(2,1)}), bf16[16,24,128]{2,1,0:T(8,128)(2,1)S(1)}, u32[]{:S(2)}, u32[]{:S(2)}) %all-to-all-start) | async-done | bytes 98336 | tf_op jit(solution)/shard_map/all_to_all | solution.py:401
  (121 shorter events, 23.8 us)
Async XLA Ops:
  1.7 14.1 %collective-permute-start.15 = (bf16[64,2688]{1,0:T(8,128)(2,1)S(1)}, bf16[64,2688]{1,0:T(8,128)(2,1)S(1)}, u32[]{:S(2)}, u32[]{:S(2)}) collective-permute-start(bf16[64,2688]{1,0:T(8,128)(2,1)S(1)} %constant_dynamic-slice_fusion), channel_id=1, source_target_pairs={{0,4},{1,5},{2,6},{3,7},{4,8},{5,9},{6,10},{7,11},{8,12},{9,13},{1... | collective-permute-start | bytes 1032200 | tf_op jit(solution)/shard_map/ppermute | solution.py:46
  4.8 17.0 %collective-permute-start.23 = (bf16[64,2688]{1,0:T(8,128)(2,1)S(1)}, bf16[64,2688]{1,0:T(8,128)(2,1)}, u32[]{:S(2)}, u32[]{:S(2)}) collective-permute-start(bf16[64,2688]{1,0:T(8,128)(2,1)S(1)} %constant_dynamic-slice_fusion), channel_id=1, source_target_pairs={{0,12},{1,13},{2,14},{3,15},{4,0},{5,1},{6,2},{7,3},{8,4},{9,5},{1... | collective-permute-start | bytes 1032200 | tf_op jit(solution)/shard_map/ppermute | solution.py:46
  6.9 26.1 %collective-permute-start.1 = (bf16[256,1024]{1,0:T(8,128)(2,1)}, bf16[256,1024]{1,0:T(8,128)(2,1)S(1)}, u32[]{:S(2)}, u32[]{:S(2)}) collective-permute-start(bf16[256,1024]{1,0:T(8,128)(2,1)} %refs_0_.3), channel_id=1, source_target_pairs={{0,4},{1,5},{2,6},{3,7},{4,8},{5,9},{6,10},{7,11},{8,12},{9,13},{1... | collective-permute-start | bytes 1572872 | tf_op jit(solution)/shard_map/ppermute | solution.py:46
  8.8 34.5 %collective-permute-start.6 = (bf16[256,1024]{1,0:T(8,128)(2,1)}, bf16[256,1024]{1,0:T(8,128)(2,1)S(1)}, u32[]{:S(2)}, u32[]{:S(2)}) collective-permute-start(bf16[256,1024]{1,0:T(8,128)(2,1)} %refs_6_.3), channel_id=1, source_target_pairs={{0,4},{1,5},{2,6},{3,7},{4,8},{5,9},{6,10},{7,11},{8,12},{9,13},{1... | collective-permute-start | bytes 1572872 | tf_op jit(solution)/shard_map/ppermute | solution.py:46
  12.3 32.5 %collective-permute-start = (bf16[256,1024]{1,0:T(8,128)(2,1)}, bf16[256,1024]{1,0:T(8,128)(2,1)S(1)}, u32[]{:S(2)}, u32[]{:S(2)}) collective-permute-start(bf16[256,1024]{1,0:T(8,128)(2,1)} %refs_0_.3), channel_id=1, source_target_pairs={{0,1},{2,3},{4,5},{6,7},{8,9},{10,11},{12,13},{14,15},{16,17},{18,... | collective-permute-start | bytes 1572872 | tf_op jit(solution)/shard_map/ppermute | solution.py:46
  15.8 30.5 %collective-permute-start.5 = (bf16[256,1024]{1,0:T(8,128)(2,1)}, bf16[256,1024]{1,0:T(8,128)(2,1)S(1)}, u32[]{:S(2)}, u32[]{:S(2)}) collective-permute-start(bf16[256,1024]{1,0:T(8,128)(2,1)} %refs_6_.3), channel_id=1, source_target_pairs={{0,1},{2,3},{4,5},{6,7},{8,9},{10,11},{12,13},{14,15},{16,17},{18,... | collective-permute-start | bytes 1572872 | tf_op jit(solution)/shard_map/ppermute | solution.py:46
  31.3 18.1 %collective-permute-start.31 = (bf16[64,2688]{1,0:T(8,128)(2,1)S(1)}, bf16[64,2688]{1,0:T(8,128)(2,1)}, u32[]{:S(2)}, u32[]{:S(2)}) collective-permute-start(bf16[64,2688]{1,0:T(8,128)(2,1)S(1)} %collective-permute-done.15.refs_8_), channel_id=1, source_target_pairs={{0,4},{1,5},{2,6},{3,7},{4,8},{5,9},{6,10},{7,11},{8,12},{9,13},{1... | collective-permute-start | bytes 1032200 | tf_op jit(solution)/shard_map/ppermute | solution.py:46
  33.0 16.4 %collective-permute-start.19 = (bf16[64,2688]{1,0:T(8,128)(2,1)S(1)}, bf16[64,2688]{1,0:T(8,128)(2,1)}, u32[]{:S(2)}, u32[]{:S(2)}) collective-permute-start(bf16[64,2688]{1,0:T(8,128)(2,1)S(1)} %collective-permute-done.15.refs_8_), channel_id=1, source_target_pairs={{0,2},{1,3},{2,0},{3,1},{4,6},{5,7},{6,4},{7,5},{8,10},{9,11},{10,... | collective-permute-start | bytes 1032200 | tf_op jit(solution)/shard_map/ppermute | solution.py:46
  44.8 10.9 %collective-permute-start.16 = (bf16[64,2688]{1,0:T(8,128)(2,1)S(1)}, bf16[64,2688]{1,0:T(8,128)(2,1)S(1)}, u32[]{:S(2)}, u32[]{:S(2)}) collective-permute-start(bf16[64,2688]{1,0:T(8,128)(2,1)S(1)} %collective-permute-done.15.refs_8_), channel_id=1, source_target_pairs={{0,16},{16,0},{1,17},{17,1},{2,18},{18,2},{3,19},{19,3},{4,20},{20... | collective-permute-start | bytes 1032200 | tf_op jit(solution)/shard_map/ppermute | solution.py:314
  46.3 16.8 %collective-permute-start.24 = (bf16[64,2688]{1,0:T(8,128)(2,1)}, bf16[64,2688]{1,0:T(8,128)(2,1)S(1)}, u32[]{:S(2)}, u32[]{:S(2)}) collective-permute-start(bf16[64,2688]{1,0:T(8,128)(2,1)} %collective-permute-done.23.refs_16_), channel_id=1, source_target_pairs={{0,16},{16,0},{1,17},{17,1},{2,18},{18,2},{3,19},{19,3},{4,20},{20... | collective-permute-start | bytes 1032200 | tf_op jit(solution)/shard_map/ppermute | solution.py:314
  49.4 21.1 %collective-permute-start.10 = (bf16[128,2688]{1,0:T(8,128)(2,1)}, bf16[128,2688]{1,0:T(8,128)(2,1)S(1)}, u32[]{:S(2)}, u32[]{:S(2)}) collective-permute-start(bf16[128,2688]{1,0:T(8,128)(2,1)} %refs_2_.1), channel_id=1, source_target_pairs={{0,1},{1,0},{2,3},{3,2},{4,5},{5,4},{6,7},{7,6},{8,9},{9,8},{10,11... | collective-permute-start | bytes 2064392 | tf_op jit(solution)/shard_map/ppermute | solution.py:46
  49.4 13.7 %collective-permute-start.17 = (bf16[64,2688]{1,0:T(8,128)(2,1)S(1)}, bf16[64,2688]{1,0:T(8,128)(2,1)S(1)}, u32[]{:S(2)}, u32[]{:S(2)}) collective-permute-start(bf16[64,2688]{1,0:T(8,128)(2,1)S(1)} %collective-permute-done.15.refs_8_), channel_id=1, source_target_pairs={{0,1},{1,0},{2,3},{3,2},{4,5},{5,4},{6,7},{7,6},{8,9},{9,8},{10,11... | collective-permute-start | bytes 1032200 | tf_op jit(solution)/shard_map/ppermute | solution.py:46
  51.3 15.9 %collective-permute-start.12 = (bf16[64,2688]{1,0:T(8,128)(2,1)}, bf16[64,2688]{1,0:T(8,128)(2,1)}, u32[]{:S(2)}, u32[]{:S(2)}) collective-permute-start(bf16[64,2688]{1,0:T(8,128)(2,1)} %collective-permute-done.11.refs_4_), channel_id=1, source_target_pairs={{0,16},{16,0},{1,17},{17,1},{2,18},{18,2},{3,19},{19,3},{4,20},{20... | collective-permute-start | bytes 1032200 | tf_op jit(solution)/shard_map/ppermute | solution.py:314
  55.7 13.0 %collective-permute-start.25 = (bf16[64,2688]{1,0:T(8,128)(2,1)}, bf16[64,2688]{1,0:T(8,128)(2,1)}, u32[]{:S(2)}, u32[]{:S(2)}) collective-permute-start(bf16[64,2688]{1,0:T(8,128)(2,1)} %collective-permute-done.23.refs_16_), channel_id=1, source_target_pairs={{0,1},{1,0},{2,3},{3,2},{4,5},{5,4},{6,7},{7,6},{8,9},{9,8},{10,11... | collective-permute-start | bytes 1032200 | tf_op jit(solution)/shard_map/ppermute | solution.py:46
  68.7 17.5 %collective-permute-start.33 = (bf16[64,2688]{1,0:T(8,128)(2,1)}, bf16[64,2688]{1,0:T(8,128)(2,1)S(1)}, u32[]{:S(2)}, u32[]{:S(2)}) collective-permute-start(bf16[64,2688]{1,0:T(8,128)(2,1)} %collective-permute-done.31.refs_24_), channel_id=1, source_target_pairs={{0,1},{1,0},{2,3},{3,2},{4,5},{5,4},{6,7},{7,6},{8,9},{9,8},{10,11... | collective-permute-start | bytes 1032200 | tf_op jit(solution)/shard_map/ppermute | solution.py:46
  68.8 15.9 %collective-permute-start.20 = (bf16[64,2688]{1,0:T(8,128)(2,1)}, bf16[64,2688]{1,0:T(8,128)(2,1)}, u32[]{:S(2)}, u32[]{:S(2)}) collective-permute-start(bf16[64,2688]{1,0:T(8,128)(2,1)} %collective-permute-done.19.refs_12_), channel_id=1, source_target_pairs={{0,16},{16,0},{1,17},{17,1},{2,18},{18,2},{3,19},{19,3},{4,20},{20... | collective-permute-start | bytes 1032200 | tf_op jit(solution)/shard_map/ppermute | solution.py:314
  70.5 19.0 %collective-permute-start.21 = (bf16[64,2688]{1,0:T(8,128)(2,1)}, bf16[64,2688]{1,0:T(8,128)(2,1)S(1)}, u32[]{:S(2)}, u32[]{:S(2)}) collective-permute-start(bf16[64,2688]{1,0:T(8,128)(2,1)} %collective-permute-done.19.refs_12_), channel_id=1, source_target_pairs={{0,1},{1,0},{2,3},{3,2},{4,5},{5,4},{6,7},{7,6},{8,9},{9,8},{10,11... | collective-permute-start | bytes 1032200 | tf_op jit(solution)/shard_map/ppermute | solution.py:46
  73.9 15.5 %collective-permute-start.28 = (bf16[64,2688]{1,0:T(8,128)(2,1)S(1)}, bf16[64,2688]{1,0:T(8,128)(2,1)}, u32[]{:S(2)}, u32[]{:S(2)}) collective-permute-start(bf16[64,2688]{1,0:T(8,128)(2,1)S(1)} %copy-done.12), channel_id=1, source_target_pairs={{0,16},{16,0},{1,17},{17,1},{2,18},{18,2},{3,19},{19,3},{4,20},{20... | collective-permute-start | bytes 1032200 | tf_op jit(solution)/shard_map/ppermute | solution.py:314
  77.3 12.8 %collective-permute-start.18 = (bf16[64,2688]{1,0:T(8,128)(2,1)S(1)}, bf16[64,2688]{1,0:T(8,128)(2,1)S(1)}, u32[]{:S(2)}, u32[]{:S(2)}) collective-permute-start(bf16[64,2688]{1,0:T(8,128)(2,1)S(1)} %copy-done.14), channel_id=1, source_target_pairs={{0,1},{1,0},{2,3},{3,2},{4,5},{5,4},{6,7},{7,6},{8,9},{9,8},{10,11... | collective-permute-start | bytes 1032200 | tf_op jit(solution)/shard_map/ppermute | solution.py:46
  84.7 14.5 %collective-permute-start.3 = (bf16[256,1024]{1,0:T(8,128)(2,1)S(1)}, bf16[256,1024]{1,0:T(8,128)(2,1)S(1)}, u32[]{:S(2)}, u32[]{:S(2)}) collective-permute-start(bf16[256,1024]{1,0:T(8,128)(2,1)S(1)} %broadcast_select_fusion.1), channel_id=1, source_target_pairs={{0,2},{1,3},{2,0},{3,1},{4,6},{5,7},{6,4},{7,5},{8,10},{9,11},{10,... | collective-permute-start | bytes 1572872 | tf_op jit(solution)/shard_map/ppermute | solution.py:46
  86.2 18.6 %collective-permute-start.8 = (bf16[256,1024]{1,0:T(8,128)(2,1)S(1)}, bf16[256,1024]{1,0:T(8,128)(2,1)S(1)}, u32[]{:S(2)}, u32[]{:S(2)}) collective-permute-start(bf16[256,1024]{1,0:T(8,128)(2,1)S(1)} %broadcast_select_fusion), channel_id=1, source_target_pairs={{0,2},{1,3},{2,0},{3,1},{4,6},{5,7},{6,4},{7,5},{8,10},{9,11},{10,... | collective-permute-start | bytes 1572872 | tf_op jit(solution)/shard_map/ppermute | solution.py:46
  90.1 14.8 %collective-permute-start.14 = (bf16[64,2688]{1,0:T(8,128)(2,1)}, bf16[64,2688]{1,0:T(8,128)(2,1)}, u32[]{:S(2)}, u32[]{:S(2)}) collective-permute-start(bf16[64,2688]{1,0:T(8,128)(2,1)} %collective-permute-done.12.refs_5_), channel_id=1, source_target_pairs={{0,1},{1,0},{2,3},{3,2},{4,5},{5,4},{6,7},{7,6},{8,9},{9,8},{10,11... | collective-permute-start | bytes 1032200 | tf_op jit(solution)/shard_map/ppermute | solution.py:46
  91.3 16.0 %collective-permute-start.2 = (bf16[256,1024]{1,0:T(8,128)(2,1)S(1)}, bf16[256,1024]{1,0:T(8,128)(2,1)S(1)}, u32[]{:S(2)}, u32[]{:S(2)}) collective-permute-start(bf16[256,1024]{1,0:T(8,128)(2,1)S(1)} %collective-permute-done.1.refs_2_), channel_id=1, source_target_pairs={{1,0},{3,2},{5,4},{7,6},{9,8},{11,10},{13,12},{15,14},{17,16},{19,... | collective-permute-start | bytes 1572872 | tf_op jit(solution)/shard_map/ppermute | solution.py:46
  92.6 14.9 %collective-permute-start.7 = (bf16[256,1024]{1,0:T(8,128)(2,1)S(1)}, bf16[256,1024]{1,0:T(8,128)(2,1)S(1)}, u32[]{:S(2)}, u32[]{:S(2)}) collective-permute-start(bf16[256,1024]{1,0:T(8,128)(2,1)S(1)} %collective-permute-done.6.refs_8_), channel_id=1, source_target_pairs={{1,0},{3,2},{5,4},{7,6},{9,8},{11,10},{13,12},{15,14},{17,16},{19,... | collective-permute-start | bytes 1572872 | tf_op jit(solution)/shard_map/ppermute | solution.py:46
  99.1 16.4 %collective-permute-start.4 = (bf16[256,1024]{1,0:T(8,128)(2,1)S(1)}, bf16[256,1024]{1,0:T(8,128)(2,1)}, u32[]{:S(2)}, u32[]{:S(2)}) collective-permute-start(bf16[256,1024]{1,0:T(8,128)(2,1)S(1)} %collective-permute-done.3.refs_4_), channel_id=1, source_target_pairs={{0,1},{1,0},{2,3},{3,2},{4,5},{5,4},{6,7},{7,6},{8,9},{9,8},{10,11... | collective-permute-start | bytes 1572872 | tf_op jit(solution)/shard_map/ppermute | solution.py:46
  104.8 11.3 %collective-permute-start.9 = (bf16[256,1024]{1,0:T(8,128)(2,1)S(1)}, bf16[256,1024]{1,0:T(8,128)(2,1)}, u32[]{:S(2)}, u32[]{:S(2)}) collective-permute-start(bf16[256,1024]{1,0:T(8,128)(2,1)S(1)} %collective-permute-done.8.refs_10_), channel_id=1, source_target_pairs={{0,1},{1,0},{2,3},{3,2},{4,5},{5,4},{6,7},{7,6},{8,9},{9,8},{10,11... | collective-permute-start | bytes 1572872 | tf_op jit(solution)/shard_map/ppermute | solution.py:46
  107.3 22.3 %collective-permute-start.37 = (bf16[64,2688]{1,0:T(8,128)(2,1)}, bf16[64,2688]{1,0:T(8,128)(2,1)S(1)}, u32[]{:S(2)}, u32[]{:S(2)}) collective-permute-start(bf16[64,2688]{1,0:T(8,128)(2,1)} %collective-permute-done.35.refs_28_), channel_id=1, source_target_pairs={{0,1},{1,0},{2,3},{3,2},{4,5},{5,4},{6,7},{7,6},{8,9},{9,8},{10,11... | collective-permute-start | bytes 1032200 | tf_op jit(solution)/shard_map/ppermute | solution.py:46
  107.5 22.1 %collective-permute-start.34 = (bf16[64,2688]{1,0:T(8,128)(2,1)}, bf16[64,2688]{1,0:T(8,128)(2,1)S(1)}, u32[]{:S(2)}, u32[]{:S(2)}) collective-permute-start(bf16[64,2688]{1,0:T(8,128)(2,1)} %collective-permute-done.32.refs_25_), channel_id=1, source_target_pairs={{0,1},{1,0},{2,3},{3,2},{4,5},{5,4},{6,7},{7,6},{8,9},{9,8},{10,11... | collective-permute-start | bytes 1032200 | tf_op jit(solution)/shard_map/ppermute | solution.py:46
  115.5 14.1 %collective-permute-start.22 = (bf16[64,2688]{1,0:T(8,128)(2,1)}, bf16[64,2688]{1,0:T(8,128)(2,1)S(1)}, u32[]{:S(2)}, u32[]{:S(2)}) collective-permute-start(bf16[64,2688]{1,0:T(8,128)(2,1)} %collective-permute-done.20.refs_13_), channel_id=1, source_target_pairs={{0,1},{1,0},{2,3},{3,2},{4,5},{5,4},{6,7},{7,6},{8,9},{9,8},{10,11... | collective-permute-start | bytes 1032200 | tf_op jit(solution)/shard_map/ppermute | solution.py:46
  115.6 14.1 %collective-permute-start.30 = (bf16[64,2688]{1,0:T(8,128)(2,1)}, bf16[64,2688]{1,0:T(8,128)(2,1)}, u32[]{:S(2)}, u32[]{:S(2)}) collective-permute-start(bf16[64,2688]{1,0:T(8,128)(2,1)} %collective-permute-done.28.refs_21_), channel_id=1, source_target_pairs={{0,1},{1,0},{2,3},{3,2},{4,5},{5,4},{6,7},{7,6},{8,9},{9,8},{10,11... | collective-permute-start | bytes 1032200 | tf_op jit(solution)/shard_map/ppermute | solution.py:46
  116.1 13.6 %collective-permute-start.38 = (bf16[64,2688]{1,0:T(8,128)(2,1)S(1)}, bf16[64,2688]{1,0:T(8,128)(2,1)}, u32[]{:S(2)}, u32[]{:S(2)}) collective-permute-start(bf16[64,2688]{1,0:T(8,128)(2,1)S(1)} %collective-permute-done.36.refs_29_), channel_id=1, source_target_pairs={{0,1},{1,0},{2,3},{3,2},{4,5},{5,4},{6,7},{7,6},{8,9},{9,8},{10,11... | collective-permute-start | bytes 1032200 | tf_op jit(solution)/shard_map/ppermute | solution.py:46
  140.0 20.2 %all-to-all-start = ((bf16[16,24,128]{2,1,0:T(8,128)(2,1)}), bf16[16,24,128]{2,1,0:T(8,128)(2,1)S(1)}, u32[]{:S(2)}, u32[]{:S(2)}) async-start(bf16[16,24,128]{2,1,0:T(8,128)(2,1)} %get-tuple-element.7), calls=%async_computation | async-start | bytes 196608 | tf_op jit(solution)/shard_map/all_to_all | solution.py:401
  (36 other events, 638.3 us)

commit v2 on v1

v2 whole, which is shorter than its diff:
```python
import math

import jax
import jax.numpy as jnp
from jax import lax
from jax.experimental import pallas as pl
from jax.experimental.pallas import tpu as pltpu
from jax.sharding import PartitionSpec as P


HEAD_FEATURES = 128
WINDOW_SPAN = 1024
SLOTS = 2
LANES = 128
UNUSED = 2**30

query_scale = 168.0 ** (-0.5)
norm_eps = 1e-06


def chip_grid(mesh):
    devices = mesh.devices.reshape(mesh.shape["groups"], mesh.shape["seq"])
    where = [(*d.coords, d.core_on_chip) for d in devices[0]]
    xs = len({w[0] for w in where})
    zs = len({w[2] for w in where})
    if xs * zs * 2 != len(where):
        return None
    return zs, xs


def passed_along(block, axis, distance):
    devices = range(lax.axis_size(axis))
    route = [(i - distance, i) for i in devices if i - distance in devices]
    return lax.ppermute(block, axis, route)


def moved(block, grid, step):
    zs, xs = grid
    route = []
    for z in range(zs):
        for x in range(xs):
            for c in range(2):
                to = step(z, x, c)
                if to is not None:
                    route.append(((z * xs + x) * 2 + c, (to[0] * xs + to[1]) * 2 + to[2]))
    return lax.ppermute(block, "seq", route)


def last_start_at(pos, prev, s0, s1):
    last = jnp.maximum(prev, jnp.where(s0 <= pos, s0, 0))
    return jnp.maximum(last, jnp.where(s1 <= pos, s1, 0))


def my_docs(starts_ref, my_index, rows):
    def one(device, prev):
        end = (device + 1) * rows
        for t in range(SLOTS):
            start = starts_ref[device * SLOTS + t]
            prev = jnp.maximum(prev, jnp.where(start < end, start, 0))
        return prev

    prev = lax.fori_loop(0, my_index, one, 0)
    end = (my_index + 1) * rows
    mine = [starts_ref[my_index * SLOTS + t] for t in range(SLOTS)]
    return [prev] + [jnp.where(start < end, start, UNUSED) for start in mine]


def attend(index, doc_starts, queries, key_blocks, value_blocks, block_at, lower, upper):
    rows, width = queries.shape
    kv_width = key_blocks[0].shape[1]
    each = width // kv_width
    count = len(key_blocks)
    tall = each * rows
    to_exp2 = query_scale * math.log2(math.e)
    heads = upper - lower
    narrow = heads * HEAD_FEATURES
    wide = each * narrow

    def kernel(index_ref, starts_ref, q_hbm, *refs):
        k_hbms, v_hbms = refs[:count], refs[count : 2 * count]
        out_ref, bias, s_ref, m_ref, l_ref, acc, q_ref, k_ref, v_ref, sems = refs[2 * count :]
        my_index = index_ref[0]
        first = my_index * rows
        prev, s0, s1 = my_docs(starts_ref, my_index, rows)
        lowest = jnp.maximum(last_start_at(first, prev, s0, s1), first - WINDOW_SPAN + 1)
        places = []
        for b in range(count):
            at, valid = block_at(b, my_index)
            start = at * rows
            places.append((start, valid & (at >= 0) & (start + rows > lowest)))

        q_copy = pltpu.make_async_copy(
            q_hbm.at[:, lower * each * HEAD_FEATURES : upper * each * HEAD_FEATURES],
            q_ref,
            sems.at[2 * count],
        )
        kv_copies = [
            pltpu.make_async_copy(
                ref.at[:, lower * HEAD_FEATURES : upper * HEAD_FEATURES],
                buffer.at[b],
                sems.at[b + at],
            )
            for at, buffer, hbms in ((0, k_ref, k_hbms), (count, v_ref, v_hbms))
            for b, ref in enumerate(hbms)
        ]
        q_copy.start()
        for copies in (kv_copies[:count], kv_copies[count:]):
            for copy, (start, need) in zip(copies, places):
                pl.when(need)(copy.start)

        for b, (start, need) in enumerate(places):

            @pl.when(need)
            def _():
                q_pos = first + lax.broadcasted_iota(jnp.int32, (rows, rows), 0)
                k_pos = start + lax.broadcasted_iota(jnp.int32, (rows, rows), 1)
                low = last_start_at(q_pos, prev, s0, s1)
                low = jnp.maximum(low, q_pos - WINDOW_SPAN + 1)
                visible = (k_pos >= low) & (k_pos <= q_pos)
                bias[b] = jnp.where(visible, 0.0, -jnp.inf)

        m_ref[...] = jnp.full(m_ref.shape, -jnp.inf, jnp.float32)
        l_ref[...] = jnp.zeros(l_ref.shape, jnp.float32)
        acc[...] = jnp.zeros(acc.shape, jnp.float32)

        def lanes(block):
            return [block[:, t : t + LANES] for t in range(0, rows, LANES)]

        q_copy.wait()
        for b, (start, need) in enumerate(places):

            @pl.when(need)
            def _():
                kv_copies[b].wait()
                for g in range(heads):
                    k = k_ref[b, :, g * HEAD_FEATURES : (g + 1) * HEAD_FEATURES]
                    for r in range(each):
                        at = (g * each + r) * HEAD_FEATURES
                        s = lax.dot_general(
                            q_ref[:, at : at + HEAD_FEATURES],
                            k,
                            (((1,), (1,)), ((), ())),
                            preferred_element_type=jnp.float32,
                        )
                        s = s + bias[b]
                        s_ref[b, g, r * rows : (r + 1) * rows] = s
                        top = m_ref[g, r * rows : (r + 1) * rows]
                        for part in lanes(s):
                            top = jnp.maximum(top, part)
                        m_ref[g, r * rows : (r + 1) * rows] = top

        for g in range(heads):
            peak = jnp.max(m_ref[g], axis=1, keepdims=True)
            m_ref[g] = jnp.broadcast_to(peak, (tall, LANES))

        for b, (start, need) in enumerate(places):

            @pl.when(need)
            def _():
                kv_copies[count + b].wait()
                for g in range(heads):
                    peak = m_ref[g]
                    parts = [jnp.exp2((part - peak) * to_exp2) for part in lanes(s_ref[b, g])]
                    l_ref[g] += sum(parts[1:], parts[0])
                    p = jnp.concatenate([part.astype(jnp.bfloat16) for part in parts], axis=1)
                    acc[g] += jnp.dot(
                        p,
                        v_ref[b, :, g * HEAD_FEATURES : (g + 1) * HEAD_FEATURES],
                        preferred_element_type=jnp.float32,
                    )

        for g in range(heads):
            totals = jnp.sum(l_ref[g], axis=1, keepdims=True)
            result = (acc[g] / totals).astype(jnp.bfloat16)
            for r in range(each):
                at = (g * each + r) * HEAD_FEATURES
                out_ref[:, at : at + HEAD_FEATURES] = result[r * rows : (r + 1) * rows]

    smem = pl.BlockSpec(memory_space=pltpu.MemorySpace.SMEM)
    return pl.pallas_call(
        kernel,
        in_specs=[smem, smem] + [pl.BlockSpec(memory_space=pl.ANY)] * (2 * count + 1),
        out_specs=pl.BlockSpec(memory_space=pltpu.MemorySpace.VMEM),
        scratch_shapes=[
            pltpu.VMEM((count, rows, rows), jnp.float32),
            pltpu.VMEM((count, heads, tall, rows), jnp.float32),
            pltpu.VMEM((heads, tall, LANES), jnp.float32),
            pltpu.VMEM((heads, tall, LANES), jnp.float32),
            pltpu.VMEM((heads, tall, HEAD_FEATURES), jnp.float32),
            pltpu.VMEM((rows, wide), jnp.bfloat16),
            pltpu.VMEM((count, rows, narrow), jnp.bfloat16),
            pltpu.VMEM((count, rows, narrow), jnp.bfloat16),
            pltpu.SemaphoreType.DMA((2 * count + 1,)),
        ],
        out_shape=jax.ShapeDtypeStruct((rows, wide), jnp.bfloat16),
        name="attend",
    )(index, doc_starts, queries, *key_blocks, *value_blocks)


def joined(parts, whole_ref):
    at = 0
    for ref in parts:
        whole_ref[:, at : at + ref.shape[1]] = ref[...]
        at += ref.shape[1]


def column_spans(columns):
    return [(at, min(512, columns - at)) for at in range(0, columns, 512)]


def project(index, group, doc_starts, attended, residual, post, pieces, row_at, chunk_of, slots):
    rows = attended[0].shape[0]
    width = sum(a.shape[1] for a in attended)
    columns = residual.shape[1]
    count = len(pieces)
    parts = len(attended)
    chunks = max(slots) + 1
    chunk = width // chunks
    spans = column_spans(columns)
    lines = -(-columns // (8 * LANES)) * 8
    slot_count = doc_starts.shape[0]
    seq_size = slot_count // SLOTS

    def kernel(index_ref, group_ref, starts_ref, post_ref, *refs):
        att_parts, piece_refs, res_hbm = refs[:parts], refs[parts : parts + count], refs[parts + count]
        hidden_ref, base_ref, share_ref, send_ref = refs[parts + count + 1 : parts + count + 5]
        w_ref, proj, att_ref, res_ref, row_ref, sems, res_sem = refs[parts + count + 5 :]
        my_index = index_ref[0]
        group = group_ref[0]
        spot = (my_index >> 2, (my_index >> 1) & 1, my_index & 1)
        copies = []
        for i, ref in enumerate(piece_refs):
            tall = ref.shape[0]
            at = slots[i] * chunk + row_at(i, spot, group)
            at = pl.multiple_of(at, math.gcd(tall, 16))
            copies.append(pltpu.make_async_copy(ref, w_ref.at[pl.ds(at, tall)], sems.at[i]))
        res_copy = pltpu.make_async_copy(res_hbm, res_ref, res_sem)
        for i in range(chunks):
            for copy, slot in zip(copies, slots):
                if slot == i:
                    copy.start()
        res_copy.start()
        joined(att_parts, att_ref)

        first = my_index * rows
        prev, s0, s1 = my_docs(starts_ref, my_index, rows)

        def next_start(device, least):
            end = (device + 1) * rows
            for t in range(SLOTS):
                start = starts_ref[device * SLOTS + t]
                least = jnp.minimum(least, jnp.where(start < end, start, seq_size * rows))
            return least

        beyond = lax.fori_loop(my_index + 1, seq_size, next_start, seq_size * rows)
        lengths = (jnp.minimum(s1, beyond) - s0, beyond - s1)
        lengths = [
            jnp.full((1, LANES), jnp.maximum(length, 1), jnp.int32).astype(jnp.float32)
            for length in lengths
        ]
        tails = ((s0 < UNUSED) & (s1 == UNUSED), s1 < UNUSED)
        for slot in range(SLOTS):
            tail = jnp.full((1, LANES), tails[slot].astype(jnp.int32)).astype(jnp.float32)
            share_ref[slot : slot + 1, :] = tail / lengths[slot]
        pos = first + lax.broadcasted_iota(jnp.int32, (rows, LANES), 0)
        last = last_start_at(pos, prev, s0, s1)
        masks = [m.astype(jnp.float32) for m in (last == s0, last == s1, last < first)]
        send_ref[...] = jnp.zeros(send_ref.shape, send_ref.dtype)
        row_ref[...] = jnp.zeros(row_ref.shape, jnp.float32)

        square = jnp.zeros((rows, LANES), jnp.float32)
        for i in range(chunks):
            for copy, slot in zip(copies, slots):
                if slot == i:
                    copy.wait()
            from_column = pl.multiple_of(chunk_of(i, spot) * chunk, LANES)
            att = att_ref[:, pl.ds(from_column, chunk)]
            for at, split in spans:
                part = jnp.dot(
                    att,
                    w_ref[i * chunk : (i + 1) * chunk, at : at + split],
                    preferred_element_type=jnp.float32,
                )
                if i > 0:
                    part = part + proj[:, at : at + split]
                proj[:, at : at + split] = part
                if i == chunks - 1:
                    for t in range(0, split, LANES):
                        square = square + part[:, t : t + LANES] * part[:, t : t + LANES]
        total = jnp.sum(square, axis=1, keepdims=True)
        norm = jnp.broadcast_to(lax.rsqrt(total * (1.0 / columns) + norm_eps), (rows, LANES))
        res_copy.wait()
        for at in range(0, columns, LANES):
            updated = res_ref[:, at : at + LANES].astype(jnp.float32) + (
                proj[:, at : at + LANES] * norm * post_ref[:, at : at + LANES]
            )
            hidden_ref[:, at : at + LANES] = updated.astype(jnp.bfloat16)
            sums = [jnp.sum(updated * m, axis=0, keepdims=True) for m in masks]
            for slot in range(SLOTS):
                base_ref[slot : slot + 1, at : at + LANES] = sums[slot]
            row_ref[at // LANES : at // LANES + 1, :] = sums[SLOTS]
        send_ref[lax.div(prev, rows)] = row_ref[...].astype(send_ref.dtype)
        inverse = jnp.concatenate([1.0 / length for length in lengths], axis=0)
        for at in range(0, columns, LANES):
            base_ref[:, at : at + LANES] = base_ref[:, at : at + LANES] * inverse

    whole = pl.BlockSpec(memory_space=pltpu.MemorySpace.VMEM)
    smem = pl.BlockSpec(memory_space=pltpu.MemorySpace.SMEM)
    return pl.pallas_call(
        kernel,
        in_specs=[smem, smem, smem]
        + [whole] * (parts + 1)
        + [pl.BlockSpec(memory_space=pl.ANY)] * (count + 1),
        out_specs=(whole, whole, whole, whole),
        out_shape=(
            jax.ShapeDtypeStruct((rows, columns), jnp.bfloat16),
            jax.ShapeDtypeStruct((SLOTS, columns), jnp.float32),
            jax.ShapeDtypeStruct((SLOTS, LANES), jnp.float32),
            jax.ShapeDtypeStruct((seq_size, lines, LANES), jnp.bfloat16),
        ),
        scratch_shapes=[
            pltpu.VMEM((width, columns), jnp.bfloat16),
            pltpu.VMEM((rows, columns), jnp.float32),
            pltpu.VMEM((rows, width), jnp.bfloat16),
            pltpu.VMEM((rows, columns), jnp.bfloat16),
            pltpu.VMEM((lines, LANES), jnp.float32),
            pltpu.SemaphoreType.DMA((count,)),
            pltpu.SemaphoreType.DMA,
        ],
        name="project",
    )(index, group, doc_starts, post, *attended, *pieces, residual)


def by_links(grid, groups, tok_rows, part_rows):
    return grid == (4, 2) and groups == 2 and WINDOW_SPAN == 4 * tok_rows and part_rows % 32 == 0


def body(grid, queries, keys, values, residual, out_weight, post_scale, doc_starts):
    my_index = lax.axis_index("seq")
    tok_rows = queries.shape[0]
    halo_blocks = WINDOW_SPAN // tok_rows
    part_rows = out_weight.shape[0]
    kv_heads = keys.shape[1] // HEAD_FEATURES

    index = my_index.reshape(1).astype(jnp.int32)
    group = lax.axis_index("groups").reshape(1).astype(jnp.int32)
    post = post_scale[None, :]

    if by_links(grid, lax.axis_size("groups"), tok_rows, part_rows):
        zs, _ = grid
        half_rows = part_rows // 2
        x = my_index // 2 % 2
        y = lax.axis_index("groups")

        def turned(k):
            return lambda block: moved(block, grid, lambda z, x, c: ((z + k) % zs, x, c))

        def over_x(block):
            return moved(block, grid, lambda z, x, c: (z, 1 - x, c))

        def over_c(block):
            return moved(block, grid, lambda z, x, c: (z, x, 1 - c))

        def over_y(block):
            return lax.ppermute(block, "groups", [(0, 1), (1, 0)])

        def up(block):
            return moved(block, grid, lambda z, x, c: (z + 1, x, c) if z + 1 < zs else None)

        def right(block):
            return moved(block, grid, lambda z, x, c: (z, x, 1) if c == 0 else None)

        def left(block):
            return moved(block, grid, lambda z, x, c: (z, x, 0) if c == 1 else None)

        own = lax.dynamic_slice_in_dim(out_weight, y * half_rows, half_rows)
        pieces, slots, sides = [], [], []

        def place(slot, piece, over_x, over_c, half):
            pieces.append(piece)
            slots.append(slot)
            sides.append((over_x, over_c, half))

        def place_all(slot, piece, side):
            other = over_y(piece)
            place(slot, piece, side, 0, "mine")
            place(slot, other, side, 0, "other")
            place(slot, over_c(piece), side, 1, "mine")
            place(slot, over_c(other), side, 1, "other")

        place(0, out_weight, 0, 0, "both")
        place(0, over_c(out_weight), 0, 1, "both")
        place_all(0, over_x(own), 1)
        nearest = turned(1)(own)
        for slot, k in ((1, 1), (2, 3), (3, 2)):
            ring = nearest
            if k == 2:
                ring = turned(1)(nearest)
            if k == 3:
                ring = turned(3)(own)
            place_all(slot, ring, 0)
            place_all(slot, over_x(ring), 1)

        def row_at(i, spot, group):
            side_x, side_c, half = sides[i]
            _, x, c = spot
            x, c = (1 - x if side_x else x), (1 - c if side_c else c)
            half = {"both": 0, "mine": group, "other": 1 - group}[half]
            return (x * 2 + c) * part_rows + half * half_rows

        def chunk_of(slot, spot):
            return (spot[0] + zs - (0, 1, 3, 2)[slot]) & (zs - 1)

        groups = []
        for mine in (keys, values):
            below = up(mine)
            onward = jnp.where(x == 0, mine, below)
            aside = over_x(onward)
            groups.append([mine, right(mine), below, left(below), aside, over_c(aside)])
        key_blocks, value_blocks = groups

        def block_at(b, index):
            chip, core = index >> 1, index & 1
            back = (0, 0, 2, 2, 1, 1)[b]
            place = (chip - back) * 2 + (core if b % 2 == 0 else 1 - core)
            valid = True
            if b == 1:
                valid = core == 1
            if b == 3:
                valid = core == 0
            return place, (place <= index) & valid

        attended = []
        half = kv_heads // 2
        for lower in (0, half):
            attended.append(
                attend(
                    index,
                    doc_starts,
                    queries,
                    key_blocks,
                    value_blocks,
                    block_at,
                    lower,
                    lower + half,
                )
            )
    else:
        pieces, slots = [lax.all_gather(out_weight, "seq", axis=0, tiled=True)], [0]
        key_blocks, value_blocks = [keys], [values]
        for distance in range(1, halo_blocks + 1):
            key_blocks.append(passed_along(keys, "seq", distance))
            value_blocks.append(passed_along(values, "seq", distance))

        def block_at(b, index):
            return index - b, index >= b

        def row_at(i, spot, group):
            return 0

        def chunk_of(slot, spot):
            return 0

        few = math.gcd(kv_heads, 4)
        attended = [
            attend(
                index, doc_starts, queries, key_blocks, value_blocks, block_at, lower, lower + few
            )
            for lower in range(0, kv_heads, few)
        ]

    hidden, base, share, send = project(
        index, group, doc_starts, attended, residual, post, pieces, row_at, chunk_of, slots
    )
    arrived = lax.all_to_all(send, "seq", 0, 0, tiled=True)
    carried_sum = jnp.sum(arrived.astype(jnp.float32), axis=0).reshape(-1)[: residual.shape[1]]
    pooled = base + share[:, :1] * carried_sum[None, :]
    return (hidden, pooled)


def solution(mesh):
    grid = chip_grid(mesh)
    placed = (
        P(("groups", "seq"), None),
        P(("groups", "seq"), None),
        P(("groups", "seq"), None),
        P(("groups", "seq"), None),
        P("seq", None),
        P(),
        P("groups"),
    )

    def whole(*args):
        return body(grid, *args)

    step = jax.shard_map(
        whole,
        mesh=mesh,
        in_specs=placed,
        out_specs=(P(("groups", "seq"), None), P(("groups", "seq"), None)),
        check_vma=False,
    )

    def run(queries, keys, values, residual, out_weight, post_scale, doc_starts):
        args = (queries, keys, values, residual, out_weight, post_scale, doc_starts)
        return step(*args)

    return run
```

time: 162 us -> 154 us (0.951)
  waiting for transfers between devices: 82.8 us -> 77.2 us
  other arithmetic: 5.49 us -> 2.59 us
  local copies, waits for them, and re-layouts: 3.34 us -> 5.88 us
  Pallas kernels: 20.3 us -> 18.3 us
    ppermute x32, waiting for transfers between devices: 42.9 us -> 37.4 us  [moved(): return lax.ppermute(block, 'seq', route)]
    unnamed x56 -> x62, local copies, waits for them, and re-layouts: 1.02 us -> 3.41 us
    pallas_call x3, Pallas kernels: 20.3 us -> 18.3 us  [the longest x1 9.37 us: project(): pl.pallas_call(kernel, in_specs=[smem, smem, smem] + [whole] * (parts + 1...]
    ppermute x32, starting transfers between devices: 27.2 us -> 28.9 us  [moved(): return lax.ppermute(block, 'seq', route)]
  transfers between devices with their start and end apart: 40 -> 40, of which waited for: 18 -> 17; matrix products, arithmetic and copies ran while one was open for 3% -> 2% of each run, Pallas kernels for 7% -> 6%
where the time goes in v2:
time: 154 us
  waiting for transfers between devices  77.2 us (50%)
  starting transfers between devices  48.9 us (32%)
  Pallas kernels  18.3 us (12%)
  local copies, waits for them, and re-layouts  5.88 us (4%)
  other arithmetic  2.59 us (2%)
    ppermute x32, waiting for transfers between devices, moved(): return lax.ppermute(block, 'seq', route)  37.4 us
    ppermute x7, waiting for transfers between devices, over_y(): return lax.ppermute(block, 'groups', [(0, 1), (1, 0)])  33.2 us
    ppermute x32, starting transfers between devices, moved(): return lax.ppermute(block, 'seq', route)  28.9 us
    all_to_all x1, starting transfers between devices, body(): arrived = lax.all_to_all(send, 'seq', 0, 0, tiled=True)  12.3 us
    pallas_call x1, Pallas kernels, project(): pl.pallas_call(kernel, in_specs=[smem, smem, smem] + [whole] * (parts + 1...  9.37 us
    pallas_call x2, Pallas kernels, attend(): pl.pallas_call(kernel, in_specs=[smem, smem] + [pl.BlockSpec(memory_space...  8.89 us
    ppermute x7, starting transfers between devices, over_y(): return lax.ppermute(block, 'groups', [(0, 1), (1, 0)])  7.73 us
    all_to_all x1, waiting for transfers between devices, body(): arrived = lax.all_to_all(send, 'seq', 0, 0, tiled=True)  6.58 us
  transfers between devices with their start and end apart: 40, of which 17 were waited for; matrix products, arithmetic and copies ran while one was open for 2% of the time, Pallas kernels for 6%

profile of v2, /device:TPU:0, one launch (start us, length us, event | category | flops | bytes accessed | tf_op | source)
XLA Modules:
  0.0 153.9 jit_solution(1858466668009987918)
XLA Ops:
  1.7 3.1 %collective-permute-start.15 = (bf16[64,2688]{1,0:T(8,128)(2,1)S(1)}, bf16[64,2688]{1,0:T(8,128)(2,1)S(1)}, u32[]{:S(2)}, u32[]{:S(2)}) collective-permute-start(bf16[64,2688]{1,0:T(8,128)(2,1)S(1)} %constant_dynamic-slice_fusion), channel_id=1, source_target_pairs={{0,4},{1,5},{2,6},{3,7},{4,8},{5,9},{6,10},{7,11},{8,12},{9,13},{1... | collective-permute-start | bytes 1032200 | tf_op jit(solution)/shard_map/ppermute | solution.py:46
  4.8 2.1 %collective-permute-start.23 = (bf16[64,2688]{1,0:T(8,128)(2,1)S(1)}, bf16[64,2688]{1,0:T(8,128)(2,1)}, u32[]{:S(2)}, u32[]{:S(2)}) collective-permute-start(bf16[64,2688]{1,0:T(8,128)(2,1)S(1)} %constant_dynamic-slice_fusion), channel_id=1, source_target_pairs={{0,12},{1,13},{2,14},{3,15},{4,0},{5,1},{6,2},{7,3},{8,4},{9,5},{1... | collective-permute-start | bytes 1032200 | tf_op jit(solution)/shard_map/ppermute | solution.py:46
  6.9 1.9 %collective-permute-start.6 = (bf16[256,1024]{1,0:T(8,128)(2,1)}, bf16[256,1024]{1,0:T(8,128)(2,1)S(1)}, u32[]{:S(2)}, u32[]{:S(2)}) collective-permute-start(bf16[256,1024]{1,0:T(8,128)(2,1)} %refs_6_.3), channel_id=1, source_target_pairs={{0,4},{1,5},{2,6},{3,7},{4,8},{5,9},{6,10},{7,11},{8,12},{9,13},{1... | collective-permute-start | bytes 1572872 | tf_op jit(solution)/shard_map/ppermute | solution.py:46
  8.8 3.5 %collective-permute-start.1 = (bf16[256,1024]{1,0:T(8,128)(2,1)}, bf16[256,1024]{1,0:T(8,128)(2,1)S(1)}, u32[]{:S(2)}, u32[]{:S(2)}) collective-permute-start(bf16[256,1024]{1,0:T(8,128)(2,1)} %refs_0_.3), channel_id=1, source_target_pairs={{0,4},{1,5},{2,6},{3,7},{4,8},{5,9},{6,10},{7,11},{8,12},{9,13},{1... | collective-permute-start | bytes 1572872 | tf_op jit(solution)/shard_map/ppermute | solution.py:46
  13.6 2.2 %collective-permute-done.15.refs_8_ = bf16[64,2688]{1,0:T(8,128)(2,1)S(1)} collective-permute-done((bf16[64,2688]{1,0:T(8,128)(2,1)S(1)}, bf16[64,2688]{1,0:T(8,128)(2,1)S(1)}, u32[]{:S(2)}, u32[]{:S(2)}) %collective-permute-start.15) | collective-permute-done | bytes 344096 | tf_op jit(solution)/shard_map/ppermute | solution.py:46
  17.1 4.7 %collective-permute-done.23.refs_16_ = bf16[64,2688]{1,0:T(8,128)(2,1)} collective-permute-done((bf16[64,2688]{1,0:T(8,128)(2,1)S(1)}, bf16[64,2688]{1,0:T(8,128)(2,1)}, u32[]{:S(2)}, u32[]{:S(2)}) %collective-permute-start.23) | collective-permute-done | bytes 344096 | tf_op jit(solution)/shard_map/ppermute | solution.py:46
  21.8 1.5 collective-permute-start.11
  23.3 8.0 %collective-permute-done.11.refs_4_ = bf16[64,2688]{1,0:T(8,128)(2,1)} collective-permute-done((bf16[64,2688]{1,0:T(8,128)(2,1)S(1)}, bf16[64,2688]{1,0:T(8,128)(2,1)}, u32[]{:S(2)}, u32[]{:S(2)}) %collective-permute-start.11) | collective-permute-done | bytes 344096 | tf_op jit(solution)/shard_map/ppermute | solution.py:46
  31.3 1.7 %collective-permute-start.31 = (bf16[64,2688]{1,0:T(8,128)(2,1)S(1)}, bf16[64,2688]{1,0:T(8,128)(2,1)}, u32[]{:S(2)}, u32[]{:S(2)}) collective-permute-start(bf16[64,2688]{1,0:T(8,128)(2,1)S(1)} %collective-permute-done.15.refs_8_), channel_id=1, source_target_pairs={{0,4},{1,5},{2,6},{3,7},{4,8},{5,9},{6,10},{7,11},{8,12},{9,13},{1... | collective-permute-start | bytes 1032200 | tf_op jit(solution)/shard_map/ppermute | solution.py:46
  33.0 1.5 collective-permute-start.19
  34.5 8.7 %collective-permute-done.1.refs_2_ = bf16[256,1024]{1,0:T(8,128)(2,1)S(1)} collective-permute-done((bf16[256,1024]{1,0:T(8,128)(2,1)}, bf16[256,1024]{1,0:T(8,128)(2,1)S(1)}, u32[]{:S(2)}, u32[]{:S(2)}) %collective-permute-start.1) | collective-permute-done | bytes 524320 | tf_op jit(solution)/shard_map/ppermute | solution.py:46
  43.3 1.5 collective-permute-start.27
  44.8 1.5 collective-permute-start.16
  46.8 2.6 %collective-permute-done.31.refs_24_ = bf16[64,2688]{1,0:T(8,128)(2,1)} collective-permute-done((bf16[64,2688]{1,0:T(8,128)(2,1)S(1)}, bf16[64,2688]{1,0:T(8,128)(2,1)}, u32[]{:S(2)}, u32[]{:S(2)}) %collective-permute-start.31) | collective-permute-done | bytes 344096 | tf_op jit(solution)/shard_map/ppermute | solution.py:46
  51.3 1.5 collective-permute-start.12
  52.8 2.9 %collective-permute-done.16.refs_9_ = bf16[64,2688]{1,0:T(8,128)(2,1)S(1)} collective-permute-done((bf16[64,2688]{1,0:T(8,128)(2,1)S(1)}, bf16[64,2688]{1,0:T(8,128)(2,1)S(1)}, u32[]{:S(2)}, u32[]{:S(2)}) %collective-permute-start.16) | collective-permute-done | bytes 344096 | tf_op jit(solution)/shard_map/ppermute | solution.py:365
  55.7 7.4 %collective-permute-done.24.refs_17_ = bf16[64,2688]{1,0:T(8,128)(2,1)S(1)} collective-permute-done((bf16[64,2688]{1,0:T(8,128)(2,1)}, bf16[64,2688]{1,0:T(8,128)(2,1)S(1)}, u32[]{:S(2)}, u32[]{:S(2)}) %collective-permute-start.24) | collective-permute-done | bytes 344096 | tf_op jit(solution)/shard_map/ppermute | solution.py:365
  65.1 2.1 %collective-permute-done.12.refs_5_ = bf16[64,2688]{1,0:T(8,128)(2,1)} collective-permute-done((bf16[64,2688]{1,0:T(8,128)(2,1)}, bf16[64,2688]{1,0:T(8,128)(2,1)}, u32[]{:S(2)}, u32[]{:S(2)}) %collective-permute-start.12) | collective-permute-done | bytes 344096 | tf_op jit(solution)/shard_map/ppermute | solution.py:365
  67.2 1.5 collective-permute-start.32
  70.6 4.0 %collective-permute-done.35.refs_28_ = bf16[64,2688]{1,0:T(8,128)(2,1)} collective-permute-done((bf16[64,2688]{1,0:T(8,128)(2,1)}, bf16[64,2688]{1,0:T(8,128)(2,1)}, u32[]{:S(2)}, u32[]{:S(2)}) %collective-permute-start.35) | collective-permute-done | bytes 344096 | tf_op jit(solution)/shard_map/ppermute | solution.py:46
  74.6 1.5 collective-permute-start.28
  76.2 1.6 %collective-permute-done.32.refs_25_ = bf16[64,2688]{1,0:T(8,128)(2,1)} collective-permute-done((bf16[64,2688]{1,0:T(8,128)(2,1)}, bf16[64,2688]{1,0:T(8,128)(2,1)}, u32[]{:S(2)}, u32[]{:S(2)}) %collective-permute-start.32) | collective-permute-done | bytes 344096 | tf_op jit(solution)/shard_map/ppermute | solution.py:365
  78.9 6.3 %collective-permute-done.20.refs_13_ = bf16[64,2688]{1,0:T(8,128)(2,1)} collective-permute-done((bf16[64,2688]{1,0:T(8,128)(2,1)}, bf16[64,2688]{1,0:T(8,128)(2,1)}, u32[]{:S(2)}, u32[]{:S(2)}) %collective-permute-start.20) | collective-permute-done | bytes 344096 | tf_op jit(solution)/shard_map/ppermute | solution.py:365
  86.4 3.3 %collective-permute-done.28.refs_21_ = bf16[64,2688]{1,0:T(8,128)(2,1)} collective-permute-done((bf16[64,2688]{1,0:T(8,128)(2,1)S(1)}, bf16[64,2688]{1,0:T(8,128)(2,1)}, u32[]{:S(2)}, u32[]{:S(2)}) %collective-permute-start.28) | collective-permute-done | bytes 344096 | tf_op jit(solution)/shard_map/ppermute | solution.py:365
  95.3 4.7 %collective-permute-done.3.refs_4_ = bf16[256,1024]{1,0:T(8,128)(2,1)S(1)} collective-permute-done((bf16[256,1024]{1,0:T(8,128)(2,1)S(1)}, bf16[256,1024]{1,0:T(8,128)(2,1)S(1)}, u32[]{:S(2)}, u32[]{:S(2)}) %collective-permute-start.3) | collective-permute-done | bytes 524320 | tf_op jit(solution)/shard_map/ppermute | solution.py:46
  101.2 9.7 %collective-permute-done.36.refs_29_ = bf16[64,2688]{1,0:T(8,128)(2,1)} collective-permute-done((bf16[64,2688]{1,0:T(8,128)(2,1)}, bf16[64,2688]{1,0:T(8,128)(2,1)}, u32[]{:S(2)}, u32[]{:S(2)}) %collective-permute-start.36) | collective-permute-done | bytes 344096 | tf_op jit(solution)/shard_map/ppermute | solution.py:365
  113.6 4.3 %attend.3.refs_1_ = bf16[256,1024]{1,0:T(8,128)(2,1)} custom-call(s32[1]{0:T(128)} %bitcast.index_ref, s32[32]{0:T(128)} %starts_ref.5, bf16[256,2048]{1,0:T(8,128)(2,1)} %q_hbm.3, bf16[256,1024]{1,0:T(8,128)(2,1)} %refs_0_.3, bf16[256,1024]{1,0:T(8,128)(2,1)} %copy-done.3, bf16[256,1024]{1,0:T(8,128)(2,1)} %copy-done.2, bf16[256,1024]{1,0:T(8,128)(2,1)} %copy-done.7, ...), custom_call_target="tpu_custom_call" | custom-call | tf_op jit(solution)/shard_map/attend/pallas_call | solution.py:180
  118.0 4.5 %attend.2.refs_0_ = bf16[256,1024]{1,0:T(8,128)(2,1)} custom-call(s32[1]{0:T(128)} %bitcast.index_ref, s32[32]{0:T(128)} %starts_ref.5, bf16[256,2048]{1,0:T(8,128)(2,1)} %q_hbm.3, bf16[256,1024]{1,0:T(8,128)(2,1)} %refs_0_.3, bf16[256,1024]{1,0:T(8,128)(2,1)} %copy-done.3, bf16[256,1024]{1,0:T(8,128)(2,1)} %copy-done.2, bf16[256,1024]{1,0:T(8,128)(2,1)} %copy-done.7, ...), custom_call_target="tpu_custom_call" | custom-call | tf_op jit(solution)/shard_map/attend/pallas_call | solution.py:180
  123.4 9.4 %project.1 = (bf16[256,2688]{1,0:T(8,128)(2,1)}, f32[2,2688]{1,0:T(2,128)}, f32[2,128]{1,0:T(2,128)}, bf16[16,24,128]{2,1,0:T(8,128)(2,1)}) custom-call(s32[1]{0:T(128)} %bitcast.index_ref, s32[1]{0:T(128)} %bitcast.1.group_ref, s32[32]{0:T(128)} %starts_ref.5, f32[1,2688]{1,0:T(1,128)} %broadcast_in_dim.4.post_ref, bf16[256,1024]{1,0:T(8,128)(2,1)} %attend.2.refs_0_, ...), custom_call_target="tpu_custom_call" | custom-call | tf_op jit(solution)/shard_map/project/pallas_call | solution.py:309
  132.8 12.3 %all-to-all-start = ((bf16[16,24,128]{2,1,0:T(8,128)(2,1)}), bf16[16,24,128]{2,1,0:T(8,128)(2,1)S(1)}, u32[]{:S(2)}, u32[]{:S(2)}) async-start(bf16[16,24,128]{2,1,0:T(8,128)(2,1)} %get-tuple-element.9), calls=%async_computation | async-start | bytes 196608 | tf_op jit(solution)/shard_map/all_to_all | solution.py:475
  145.9 6.6 %all-to-all-done = bf16[16,24,128]{2,1,0:T(8,128)(2,1)S(1)} async-done(((bf16[16,24,128]{2,1,0:T(8,128)(2,1)}), bf16[16,24,128]{2,1,0:T(8,128)(2,1)S(1)}, u32[]{:S(2)}, u32[]{:S(2)}) %all-to-all-start) | async-done | bytes 98336 | tf_op jit(solution)/shard_map/all_to_all | solution.py:475
  152.5 1.4 multiply_add_fusion
  (121 shorter events, 23.3 us)
Async XLA Ops:
  1.7 14.1 %collective-permute-start.15 = (bf16[64,2688]{1,0:T(8,128)(2,1)S(1)}, bf16[64,2688]{1,0:T(8,128)(2,1)S(1)}, u32[]{:S(2)}, u32[]{:S(2)}) collective-permute-start(bf16[64,2688]{1,0:T(8,128)(2,1)S(1)} %constant_dynamic-slice_fusion), channel_id=1, source_target_pairs={{0,4},{1,5},{2,6},{3,7},{4,8},{5,9},{6,10},{7,11},{8,12},{9,13},{1... | collective-permute-start | bytes 1032200 | tf_op jit(solution)/shard_map/ppermute | solution.py:46
  4.8 17.0 %collective-permute-start.23 = (bf16[64,2688]{1,0:T(8,128)(2,1)S(1)}, bf16[64,2688]{1,0:T(8,128)(2,1)}, u32[]{:S(2)}, u32[]{:S(2)}) collective-permute-start(bf16[64,2688]{1,0:T(8,128)(2,1)S(1)} %constant_dynamic-slice_fusion), channel_id=1, source_target_pairs={{0,12},{1,13},{2,14},{3,15},{4,0},{5,1},{6,2},{7,3},{8,4},{9,5},{1... | collective-permute-start | bytes 1032200 | tf_op jit(solution)/shard_map/ppermute | solution.py:46
  6.9 26.1 %collective-permute-start.6 = (bf16[256,1024]{1,0:T(8,128)(2,1)}, bf16[256,1024]{1,0:T(8,128)(2,1)S(1)}, u32[]{:S(2)}, u32[]{:S(2)}) collective-permute-start(bf16[256,1024]{1,0:T(8,128)(2,1)} %refs_6_.3), channel_id=1, source_target_pairs={{0,4},{1,5},{2,6},{3,7},{4,8},{5,9},{6,10},{7,11},{8,12},{9,13},{1... | collective-permute-start | bytes 1572872 | tf_op jit(solution)/shard_map/ppermute | solution.py:46
  8.8 34.5 %collective-permute-start.1 = (bf16[256,1024]{1,0:T(8,128)(2,1)}, bf16[256,1024]{1,0:T(8,128)(2,1)S(1)}, u32[]{:S(2)}, u32[]{:S(2)}) collective-permute-start(bf16[256,1024]{1,0:T(8,128)(2,1)} %refs_0_.3), channel_id=1, source_target_pairs={{0,4},{1,5},{2,6},{3,7},{4,8},{5,9},{6,10},{7,11},{8,12},{9,13},{1... | collective-permute-start | bytes 1572872 | tf_op jit(solution)/shard_map/ppermute | solution.py:46
  12.3 32.5 %collective-permute-start = (bf16[256,1024]{1,0:T(8,128)(2,1)}, bf16[256,1024]{1,0:T(8,128)(2,1)S(1)}, u32[]{:S(2)}, u32[]{:S(2)}) collective-permute-start(bf16[256,1024]{1,0:T(8,128)(2,1)} %refs_0_.3), channel_id=1, source_target_pairs={{0,1},{2,3},{4,5},{6,7},{8,9},{10,11},{12,13},{14,15},{16,17},{18,... | collective-permute-start | bytes 1572872 | tf_op jit(solution)/shard_map/ppermute | solution.py:46
  15.8 30.5 %collective-permute-start.5 = (bf16[256,1024]{1,0:T(8,128)(2,1)}, bf16[256,1024]{1,0:T(8,128)(2,1)S(1)}, u32[]{:S(2)}, u32[]{:S(2)}) collective-permute-start(bf16[256,1024]{1,0:T(8,128)(2,1)} %refs_6_.3), channel_id=1, source_target_pairs={{0,1},{2,3},{4,5},{6,7},{8,9},{10,11},{12,13},{14,15},{16,17},{18,... | collective-permute-start | bytes 1572872 | tf_op jit(solution)/shard_map/ppermute | solution.py:46
  31.3 18.1 %collective-permute-start.31 = (bf16[64,2688]{1,0:T(8,128)(2,1)S(1)}, bf16[64,2688]{1,0:T(8,128)(2,1)}, u32[]{:S(2)}, u32[]{:S(2)}) collective-permute-start(bf16[64,2688]{1,0:T(8,128)(2,1)S(1)} %collective-permute-done.15.refs_8_), channel_id=1, source_target_pairs={{0,4},{1,5},{2,6},{3,7},{4,8},{5,9},{6,10},{7,11},{8,12},{9,13},{1... | collective-permute-start | bytes 1032200 | tf_op jit(solution)/shard_map/ppermute | solution.py:46
  33.0 16.4 %collective-permute-start.19 = (bf16[64,2688]{1,0:T(8,128)(2,1)S(1)}, bf16[64,2688]{1,0:T(8,128)(2,1)S(1)}, u32[]{:S(2)}, u32[]{:S(2)}) collective-permute-start(bf16[64,2688]{1,0:T(8,128)(2,1)S(1)} %collective-permute-done.15.refs_8_), channel_id=1, source_target_pairs={{0,2},{1,3},{2,0},{3,1},{4,6},{5,7},{6,4},{7,5},{8,10},{9,11},{10,... | collective-permute-start | bytes 1032200 | tf_op jit(solution)/shard_map/ppermute | solution.py:46
  44.8 10.9 %collective-permute-start.16 = (bf16[64,2688]{1,0:T(8,128)(2,1)S(1)}, bf16[64,2688]{1,0:T(8,128)(2,1)S(1)}, u32[]{:S(2)}, u32[]{:S(2)}) collective-permute-start(bf16[64,2688]{1,0:T(8,128)(2,1)S(1)} %collective-permute-done.15.refs_8_), channel_id=1, source_target_pairs={{0,16},{16,0},{1,17},{17,1},{2,18},{18,2},{3,19},{19,3},{4,20},{20... | collective-permute-start | bytes 1032200 | tf_op jit(solution)/shard_map/ppermute | solution.py:365
  46.3 16.8 %collective-permute-start.24 = (bf16[64,2688]{1,0:T(8,128)(2,1)}, bf16[64,2688]{1,0:T(8,128)(2,1)S(1)}, u32[]{:S(2)}, u32[]{:S(2)}) collective-permute-start(bf16[64,2688]{1,0:T(8,128)(2,1)} %collective-permute-done.23.refs_16_), channel_id=1, source_target_pairs={{0,16},{16,0},{1,17},{17,1},{2,18},{18,2},{3,19},{19,3},{4,20},{20... | collective-permute-start | bytes 1032200 | tf_op jit(solution)/shard_map/ppermute | solution.py:365
  49.4 21.0 %collective-permute-start.10 = (bf16[128,2688]{1,0:T(8,128)(2,1)}, bf16[128,2688]{1,0:T(8,128)(2,1)S(1)}, u32[]{:S(2)}, u32[]{:S(2)}) collective-permute-start(bf16[128,2688]{1,0:T(8,128)(2,1)} %refs_2_.1), channel_id=1, source_target_pairs={{0,1},{1,0},{2,3},{3,2},{4,5},{5,4},{6,7},{7,6},{8,9},{9,8},{10,11... | collective-permute-start | bytes 2064392 | tf_op jit(solution)/shard_map/ppermute | solution.py:46
  49.4 13.7 %collective-permute-start.17 = (bf16[64,2688]{1,0:T(8,128)(2,1)S(1)}, bf16[64,2688]{1,0:T(8,128)(2,1)S(1)}, u32[]{:S(2)}, u32[]{:S(2)}) collective-permute-start(bf16[64,2688]{1,0:T(8,128)(2,1)S(1)} %collective-permute-done.15.refs_8_), channel_id=1, source_target_pairs={{0,1},{1,0},{2,3},{3,2},{4,5},{5,4},{6,7},{7,6},{8,9},{9,8},{10,11... | collective-permute-start | bytes 1032200 | tf_op jit(solution)/shard_map/ppermute | solution.py:46
  51.3 15.9 %collective-permute-start.12 = (bf16[64,2688]{1,0:T(8,128)(2,1)}, bf16[64,2688]{1,0:T(8,128)(2,1)}, u32[]{:S(2)}, u32[]{:S(2)}) collective-permute-start(bf16[64,2688]{1,0:T(8,128)(2,1)} %collective-permute-done.11.refs_4_), channel_id=1, source_target_pairs={{0,16},{16,0},{1,17},{17,1},{2,18},{18,2},{3,19},{19,3},{4,20},{20... | collective-permute-start | bytes 1032200 | tf_op jit(solution)/shard_map/ppermute | solution.py:365
  55.7 13.0 %collective-permute-start.25 = (bf16[64,2688]{1,0:T(8,128)(2,1)}, bf16[64,2688]{1,0:T(8,128)(2,1)}, u32[]{:S(2)}, u32[]{:S(2)}) collective-permute-start(bf16[64,2688]{1,0:T(8,128)(2,1)} %collective-permute-done.23.refs_16_), channel_id=1, source_target_pairs={{0,1},{1,0},{2,3},{3,2},{4,5},{5,4},{6,7},{7,6},{8,9},{9,8},{10,11... | collective-permute-start | bytes 1032200 | tf_op jit(solution)/shard_map/ppermute | solution.py:46
  64.5 10.1 %collective-permute-start.35 = (bf16[64,2688]{1,0:T(8,128)(2,1)}, bf16[64,2688]{1,0:T(8,128)(2,1)}, u32[]{:S(2)}, u32[]{:S(2)}) collective-permute-start(bf16[64,2688]{1,0:T(8,128)(2,1)} %collective-permute-done.31.refs_24_), channel_id=1, source_target_pairs={{0,2},{1,3},{2,0},{3,1},{4,6},{5,7},{6,4},{7,5},{8,10},{9,11},{10,... | collective-permute-start | bytes 1032200 | tf_op jit(solution)/shard_map/ppermute | solution.py:46
  67.2 10.7 %collective-permute-start.32 = (bf16[64,2688]{1,0:T(8,128)(2,1)}, bf16[64,2688]{1,0:T(8,128)(2,1)}, u32[]{:S(2)}, u32[]{:S(2)}) collective-permute-start(bf16[64,2688]{1,0:T(8,128)(2,1)} %collective-permute-done.31.refs_24_), channel_id=1, source_target_pairs={{0,16},{16,0},{1,17},{17,1},{2,18},{18,2},{3,19},{19,3},{4,20},{20... | collective-permute-start | bytes 1032200 | tf_op jit(solution)/shard_map/ppermute | solution.py:365
  68.7 17.6 %collective-permute-start.33 = (bf16[64,2688]{1,0:T(8,128)(2,1)}, bf16[64,2688]{1,0:T(8,128)(2,1)S(1)}, u32[]{:S(2)}, u32[]{:S(2)}) collective-permute-start(bf16[64,2688]{1,0:T(8,128)(2,1)} %collective-permute-done.31.refs_24_), channel_id=1, source_target_pairs={{0,1},{1,0},{2,3},{3,2},{4,5},{5,4},{6,7},{7,6},{8,9},{9,8},{10,11... | collective-permute-start | bytes 1032200 | tf_op jit(solution)/shard_map/ppermute | solution.py:46
  68.7 16.5 %collective-permute-start.20 = (bf16[64,2688]{1,0:T(8,128)(2,1)}, bf16[64,2688]{1,0:T(8,128)(2,1)}, u32[]{:S(2)}, u32[]{:S(2)}) collective-permute-start(bf16[64,2688]{1,0:T(8,128)(2,1)} %copy-done.13), channel_id=1, source_target_pairs={{0,16},{16,0},{1,17},{17,1},{2,18},{18,2},{3,19},{19,3},{4,20},{20... | collective-permute-start | bytes 1032200 | tf_op jit(solution)/shard_map/ppermute | solution.py:365
  70.4 19.3 %collective-permute-start.21 = (bf16[64,2688]{1,0:T(8,128)(2,1)S(1)}, bf16[64,2688]{1,0:T(8,128)(2,1)S(1)}, u32[]{:S(2)}, u32[]{:S(2)}) collective-permute-start(bf16[64,2688]{1,0:T(8,128)(2,1)S(1)} %copy-done.14), channel_id=1, source_target_pairs={{0,1},{1,0},{2,3},{3,2},{4,5},{5,4},{6,7},{7,6},{8,9},{9,8},{10,11... | collective-permute-start | bytes 1032200 | tf_op jit(solution)/shard_map/ppermute | solution.py:46
  74.6 15.1 %collective-permute-start.28 = (bf16[64,2688]{1,0:T(8,128)(2,1)S(1)}, bf16[64,2688]{1,0:T(8,128)(2,1)}, u32[]{:S(2)}, u32[]{:S(2)}) collective-permute-start(bf16[64,2688]{1,0:T(8,128)(2,1)S(1)} %copy-done.16), channel_id=1, source_target_pairs={{0,16},{16,0},{1,17},{17,1},{2,18},{18,2},{3,19},{19,3},{4,20},{20... | collective-permute-start | bytes 1032200 | tf_op jit(solution)/shard_map/ppermute | solution.py:365
  77.9 16.2 %collective-permute-start.8 = (bf16[256,1024]{1,0:T(8,128)(2,1)S(1)}, bf16[256,1024]{1,0:T(8,128)(2,1)S(1)}, u32[]{:S(2)}, u32[]{:S(2)}) collective-permute-start(bf16[256,1024]{1,0:T(8,128)(2,1)S(1)} %broadcast_select_fusion), channel_id=1, source_target_pairs={{0,2},{1,3},{2,0},{3,1},{4,6},{5,7},{6,4},{7,5},{8,10},{9,11},{10,... | collective-permute-start | bytes 1572872 | tf_op jit(solution)/shard_map/ppermute | solution.py:46
  85.2 14.8 %collective-permute-start.3 = (bf16[256,1024]{1,0:T(8,128)(2,1)S(1)}, bf16[256,1024]{1,0:T(8,128)(2,1)S(1)}, u32[]{:S(2)}, u32[]{:S(2)}) collective-permute-start(bf16[256,1024]{1,0:T(8,128)(2,1)S(1)} %broadcast_select_fusion.1), channel_id=1, source_target_pairs={{0,2},{1,3},{2,0},{3,1},{4,6},{5,7},{6,4},{7,5},{8,10},{9,11},{10,... | collective-permute-start | bytes 1572872 | tf_op jit(solution)/shard_map/ppermute | solution.py:46
  90.3 9.7 %collective-permute-start.14 = (bf16[64,2688]{1,0:T(8,128)(2,1)}, bf16[64,2688]{1,0:T(8,128)(2,1)S(1)}, u32[]{:S(2)}, u32[]{:S(2)}) collective-permute-start(bf16[64,2688]{1,0:T(8,128)(2,1)} %collective-permute-done.12.refs_5_), channel_id=1, source_target_pairs={{0,1},{1,0},{2,3},{3,2},{4,5},{5,4},{6,7},{7,6},{8,9},{9,8},{10,11... | collective-permute-start | bytes 1032200 | tf_op jit(solution)/shard_map/ppermute | solution.py:46
  94.1 16.8 %collective-permute-start.9 = (bf16[256,1024]{1,0:T(8,128)(2,1)S(1)}, bf16[256,1024]{1,0:T(8,128)(2,1)S(1)}, u32[]{:S(2)}, u32[]{:S(2)}) collective-permute-start(bf16[256,1024]{1,0:T(8,128)(2,1)S(1)} %collective-permute-done.8.refs_10_), channel_id=1, source_target_pairs={{0,1},{1,0},{2,3},{3,2},{4,5},{5,4},{6,7},{7,6},{8,9},{9,8},{10,11... | collective-permute-start | bytes 1572872 | tf_op jit(solution)/shard_map/ppermute | solution.py:46
  100.1 11.3 %collective-permute-start.4 = (bf16[256,1024]{1,0:T(8,128)(2,1)S(1)}, bf16[256,1024]{1,0:T(8,128)(2,1)S(1)}, u32[]{:S(2)}, u32[]{:S(2)}) collective-permute-start(bf16[256,1024]{1,0:T(8,128)(2,1)S(1)} %collective-permute-done.3.refs_4_), channel_id=1, source_target_pairs={{0,1},{1,0},{2,3},{3,2},{4,5},{5,4},{6,7},{7,6},{8,9},{9,8},{10,11... | collective-permute-start | bytes 1572872 | tf_op jit(solution)/shard_map/ppermute | solution.py:46
  100.1 10.8 %collective-permute-start.36 = (bf16[64,2688]{1,0:T(8,128)(2,1)}, bf16[64,2688]{1,0:T(8,128)(2,1)}, u32[]{:S(2)}, u32[]{:S(2)}) collective-permute-start(bf16[64,2688]{1,0:T(8,128)(2,1)} %collective-permute-done.35.refs_28_), channel_id=1, source_target_pairs={{0,16},{16,0},{1,17},{17,1},{2,18},{18,2},{3,19},{19,3},{4,20},{20... | collective-permute-start | bytes 1032200 | tf_op jit(solution)/shard_map/ppermute | solution.py:365
  100.6 21.9 %collective-permute-start.37 = (bf16[64,2688]{1,0:T(8,128)(2,1)}, bf16[64,2688]{1,0:T(8,128)(2,1)S(1)}, u32[]{:S(2)}, u32[]{:S(2)}) collective-permute-start(bf16[64,2688]{1,0:T(8,128)(2,1)} %collective-permute-done.35.refs_28_), channel_id=1, source_target_pairs={{0,1},{1,0},{2,3},{3,2},{4,5},{5,4},{6,7},{7,6},{8,9},{9,8},{10,11... | collective-permute-start | bytes 1032200 | tf_op jit(solution)/shard_map/ppermute | solution.py:46
  100.8 21.7 %collective-permute-start.34 = (bf16[64,2688]{1,0:T(8,128)(2,1)}, bf16[64,2688]{1,0:T(8,128)(2,1)S(1)}, u32[]{:S(2)}, u32[]{:S(2)}) collective-permute-start(bf16[64,2688]{1,0:T(8,128)(2,1)} %collective-permute-done.32.refs_25_), channel_id=1, source_target_pairs={{0,1},{1,0},{2,3},{3,2},{4,5},{5,4},{6,7},{7,6},{8,9},{9,8},{10,11... | collective-permute-start | bytes 1032200 | tf_op jit(solution)/shard_map/ppermute | solution.py:46
  110.9 11.7 %collective-permute-start.22 = (bf16[64,2688]{1,0:T(8,128)(2,1)}, bf16[64,2688]{1,0:T(8,128)(2,1)}, u32[]{:S(2)}, u32[]{:S(2)}) collective-permute-start(bf16[64,2688]{1,0:T(8,128)(2,1)} %collective-permute-done.20.refs_13_), channel_id=1, source_target_pairs={{0,1},{1,0},{2,3},{3,2},{4,5},{5,4},{6,7},{7,6},{8,9},{9,8},{10,11... | collective-permute-start | bytes 1032200 | tf_op jit(solution)/shard_map/ppermute | solution.py:46
  110.9 11.7 %collective-permute-start.30 = (bf16[64,2688]{1,0:T(8,128)(2,1)}, bf16[64,2688]{1,0:T(8,128)(2,1)}, u32[]{:S(2)}, u32[]{:S(2)}) collective-permute-start(bf16[64,2688]{1,0:T(8,128)(2,1)} %collective-permute-done.28.refs_21_), channel_id=1, source_target_pairs={{0,1},{1,0},{2,3},{3,2},{4,5},{5,4},{6,7},{7,6},{8,9},{9,8},{10,11... | collective-permute-start | bytes 1032200 | tf_op jit(solution)/shard_map/ppermute | solution.py:46
  112.4 10.1 %collective-permute-start.38 = (bf16[64,2688]{1,0:T(8,128)(2,1)}, bf16[64,2688]{1,0:T(8,128)(2,1)}, u32[]{:S(2)}, u32[]{:S(2)}) collective-permute-start(bf16[64,2688]{1,0:T(8,128)(2,1)} %collective-permute-done.36.refs_29_), channel_id=1, source_target_pairs={{0,1},{1,0},{2,3},{3,2},{4,5},{5,4},{6,7},{7,6},{8,9},{9,8},{10,11... | collective-permute-start | bytes 1032200 | tf_op jit(solution)/shard_map/ppermute | solution.py:46
  132.8 19.7 %all-to-all-start = ((bf16[16,24,128]{2,1,0:T(8,128)(2,1)}), bf16[16,24,128]{2,1,0:T(8,128)(2,1)S(1)}, u32[]{:S(2)}, u32[]{:S(2)}) async-start(bf16[16,24,128]{2,1,0:T(8,128)(2,1)} %get-tuple-element.9), calls=%async_computation | async-start | bytes 196608 | tf_op jit(solution)/shard_map/all_to_all | solution.py:475
  (39 other events, 645.8 us)
